TPU v7x, 256 devices: a whole 4x4x8 slice. The times are simulated.
256 devices in a mesh: dp: 32 (over z, y), section: 2 (over core), tensor: 4 (over x).
Axes of the slice: x: 4, y: 4, z: 8, core: 2. Of those that a mesh axis runs over, the one named last changes fastest.
Arguments:
- tokens: bfloat16 [8192, 2048], P('dp'), may hold values from -6 to 6
- base_rows: int32 [128], replicated, may hold values from 1 to 6, as said below
- baseline_owner: int32 [128], replicated, may hold values from 0 to 31, as said below
- cotangent: bfloat16 [2, 16384, 2048], P('section', 'dp'), may hold values from -6 to 6
- pre_gain: float32 [2, 2048], P('section'), may hold values from 0.25 to 1.75
- input_proj: bfloat16 [2, 2048, 2048], P('section', None, 'tensor'), may hold values from -0.125 to 0.125
- gate_proj: bfloat16 [2, 2048, 2048], P('section', None, 'tensor'), may hold values from -0.125 to 0.125
- state_proj: bfloat16 [2, 2048, 256], P('section'), may hold values from -0.125 to 0.125
- step_proj: bfloat16 [2, 2048, 32], P('section', None, 'tensor'), may hold values from -0.125 to 0.125
- step_bias: float32 [2, 32], P('section', 'tensor'), may hold values from -6 to -1.5
- decay_log: float32 [2, 32], P('section', 'tensor'), may hold values from 0 to 2.5
- skip_gain: float32 [2, 32], P('section', 'tensor'), may hold values from 0.5 to 1.5
- norm_gain: float32 [2, 2048], P('section', 'tensor'), may hold values from 0.25 to 1.75
- out_proj: bfloat16 [2, 2048, 2048], P('section', 'tensor'), may hold values from -0.125 to 0.125
Outputs:
- activations: bfloat16 [2, 16384, 2048], P('section', 'dp')
- out_grad: bfloat16 [2, 2048, 2048], P('section', 'tensor', 'dp')
Inputs may be any that keep to these rules, and one draw needn't show every extreme that they name: `base_rows`: over all baselines they sum to 256; some baseline has exactly 6. `baseline_owner`: every owner holds exactly 4 baselines; the base_rows of one owner's baselines sum to at most 16, and for some owner to exactly 16.
All inputs are finite; a program needn't handle non-finite values.
Results may differ from a plain program's by a relative error of at most 0.025.
Values may be sent and summed in bfloat16 or wider, within the bound.
A program may use at most 128 MiB of HBM per device.

v0:
```python
import jax
import jax.numpy as jnp
from jax import lax
from jax.sharding import PartitionSpec as P

HEADS = 32
HEADDIM = 64
NSTATE = 128
BLOCK = 64
MICRO = 2


EPS = 1e-05


def from_behind(value, axis, steps):
    count = lax.axis_size(axis)
    first, last = (max(0, -steps), min(count, count - steps))
    return lax.ppermute(value, axis, [(source, source + steps) for source in range(first, last)])


def layout_tables(base_rows, baseline_owner):
    count = base_rows.shape[0]
    index = jnp.arange(count, dtype=jnp.int32)
    ends = jnp.cumsum(base_rows)
    starts = ends - base_rows
    earlier = (baseline_owner[:, None] == baseline_owner[None, :]) & (
        index[None, :] < index[:, None]
    )
    owner_start = jnp.sum(jnp.where(earlier, base_rows[None, :], 0), axis=1)
    return (index, starts, ends, owner_start)


def block_scan(
    heads_in, b_rows, c_rows, step_size, decay_rate, segment, state, prev_segment, block
):
    total_rows, head_count, head_dim = heads_in.shape
    blocks = total_rows // block

    def advance(carried_in, item):
        state_now, segment_before = carried_in
        x_blk, b_blk, c_blk, dt_blk, seg_blk = item
        running = jnp.cumsum(dt_blk * decay_rate[None, :], axis=0)
        positions = jnp.arange(block, dtype=jnp.int32)
        together = (seg_blk[:, None] == seg_blk[None, :]) & (
            positions[:, None] >= positions[None, :]
        )
        spread = jnp.minimum(running[:, None, :] - running[None, :, :], 0.0)
        decay_mask = jnp.where(together[:, :, None], jnp.exp(spread), 0.0)
        scores = jnp.dot(c_blk, b_blk.T, preferred_element_type=jnp.float32)
        weights = (decay_mask * scores[:, :, None] * dt_blk[None, :, :]).astype(jnp.bfloat16)
        within = jnp.einsum("ijh,jhp->ihp", weights, x_blk, preferred_element_type=jnp.float32)
        keep_in = (seg_blk == segment_before).astype(jnp.float32)
        readout = jnp.einsum(
            "in,hpn->ihp", c_blk, state_now.astype(jnp.bfloat16), preferred_element_type=jnp.float32
        )
        from_state = keep_in[:, None, None] * jnp.exp(running)[:, :, None] * readout
        last_segment = seg_blk[-1]
        tail_weight = (
            jnp.where(
                (seg_blk == last_segment)[:, None], jnp.exp(running[-1][None, :] - running), 0.0
            )
            * dt_blk
        )
        scaled = (tail_weight[:, :, None] * x_blk.astype(jnp.float32)).astype(jnp.bfloat16)
        fresh_term = jnp.einsum("jhp,jn->hpn", scaled, b_blk, preferred_element_type=jnp.float32)
        keep_state = (last_segment == segment_before).astype(jnp.float32)
        state_next = keep_state * jnp.exp(running[-1])[:, None, None] * state_now + fresh_term
        return ((state_next, last_segment), within + from_state)

    scanned = (
        heads_in.reshape(blocks, block, head_count, head_dim),
        b_rows.reshape(blocks, block, -1),
        c_rows.reshape(blocks, block, -1),
        step_size.reshape(blocks, block, head_count),
        segment.reshape(blocks, block),
    )
    (state, prev_segment), outputs = lax.scan(advance, (state, prev_segment), scanned)
    return (outputs.reshape(total_rows, head_count, head_dim), state, prev_segment)


def block_layer(rows_in, segment, carried_state, params):
    (
        pre_gain,
        input_proj,
        gate_proj,
        state_proj,
        step_proj,
        step_bias,
        decay_log,
        skip_gain,
        norm_gain,
        out_proj,
    ) = params
    row_count = rows_in.shape[0]
    local_heads = step_proj.shape[1]
    rows_f = rows_in.astype(jnp.float32)
    normed = (
        rows_f * lax.rsqrt(jnp.mean(rows_f * rows_f, axis=-1, keepdims=True) + EPS) * pre_gain
    ).astype(jnp.bfloat16)
    scan_in = jax.nn.silu(jnp.dot(normed, input_proj, preferred_element_type=jnp.float32)).astype(
        jnp.bfloat16
    )
    gate_pre = jnp.dot(normed, gate_proj, preferred_element_type=jnp.float32)
    state_io = jax.nn.silu(jnp.dot(normed, state_proj, preferred_element_type=jnp.float32)).astype(
        jnp.bfloat16
    )
    step_size = jax.nn.softplus(
        jnp.dot(normed, step_proj, preferred_element_type=jnp.float32) + step_bias
    )
    decay_rate = -jnp.exp(decay_log)
    heads_in = scan_in.reshape(row_count, local_heads, HEADDIM)
    scan_out, state_end, segment_end = block_scan(
        heads_in,
        state_io[:, :NSTATE],
        state_io[:, NSTATE:],
        step_size,
        decay_rate,
        segment,
        carried_state[0],
        carried_state[1],
        BLOCK,
    )
    scan_out = scan_out + skip_gain[None, :, None] * heads_in.astype(jnp.float32)
    gated = scan_out.reshape(row_count, local_heads * HEADDIM) * jax.nn.silu(gate_pre)
    sq_sum = lax.psum(jnp.sum(gated * gated, axis=-1), "tensor")
    y_norm = (gated * lax.rsqrt(sq_sum[:, None] / (HEADS * HEADDIM) + EPS) * norm_gain).astype(
        jnp.bfloat16
    )
    row_share = row_count // lax.axis_size("tensor")
    summed = lax.psum_scatter(
        jnp.dot(y_norm, out_proj, preferred_element_type=jnp.float32).astype(jnp.bfloat16),
        "tensor",
        scatter_dimension=0,
        tiled=True,
    ).astype(jnp.float32)
    own_rows = lax.dynamic_slice_in_dim(rows_f, lax.axis_index("tensor") * row_share, row_share, 0)
    own_out = (own_rows + summed).astype(jnp.bfloat16)
    result = lax.all_gather(own_out, "tensor", axis=0, tiled=True)
    return (result, y_norm, (state_end, segment_end))


def grad_term(y_norm, cot_rows):
    return lax.dot_general(
        y_norm, cot_rows, (((0,), (0,)), ((), ())), preferred_element_type=jnp.float32
    )


def per_device(
    tokens,
    base_rows,
    baseline_owner,
    cotangent,
    pre_gain,
    input_proj,
    gate_proj,
    state_proj,
    step_proj,
    step_bias,
    decay_log,
    skip_gain,
    norm_gain,
    out_proj,
):
    dp_count = lax.axis_size("dp")
    tok_rows, feat_width = tokens.shape
    slot_cap = 2 * tok_rows // dp_count
    own_slots = slot_cap * dp_count
    index, starts, ends, owner_start = layout_tables(base_rows, baseline_owner)
    local = jnp.arange(tok_rows, dtype=jnp.int32)
    inside = ((starts[None, :] <= local[:, None]) & (local[:, None] < ends[None, :])).astype(
        jnp.int32
    )
    row_start = jnp.sum(inside * starts[None, :], axis=1)
    row_owner = jnp.sum(inside * baseline_owner[None, :], axis=1)
    row_ostart = jnp.sum(inside * owner_start[None, :], axis=1)
    send_slot = row_owner * slot_cap + row_ostart + local - row_start
    outgoing = (
        jnp.zeros((own_slots, feat_width), jnp.bfloat16)
        .at[send_slot]
        .set(tokens)
        .reshape(dp_count, slot_cap, feat_width)
    )
    owner_index = lax.axis_index("dp")
    place = jnp.arange(slot_cap, dtype=jnp.int32)
    held = (
        (baseline_owner[None, :] == owner_index)
        & (owner_start[None, :] <= place[:, None])
        & (place[:, None] < owner_start[None, :] + base_rows[None, :])
    ).astype(jnp.int32)
    got_start = jnp.sum(held * owner_start[None, :], axis=1)
    got_len = jnp.sum(held * base_rows[None, :], axis=1)
    got_id = jnp.sum(held * index[None, :], axis=1)
    got_any = jnp.sum(held, axis=1)
    sender = jnp.arange(dp_count, dtype=jnp.int32)[:, None]
    recv_slot = (
        dp_count * got_start[None, :]
        + sender * got_len[None, :]
        + place[None, :]
        - got_start[None, :]
    )
    recv_slot = jnp.where(got_any[None, :] > 0, recv_slot, own_slots).reshape(-1)
    id_rows = jnp.broadcast_to(got_id[None, :], (dp_count, slot_cap)).reshape(-1)
    slot_ids = jnp.full((own_slots,), -1, jnp.int32).at[recv_slot].set(id_rows, mode="drop")
    arrived = lax.all_to_all(outgoing, "dp", split_axis=0, concat_axis=0, tiled=True)
    width = arrived.shape[-1]
    stream = (
        jnp.zeros((own_slots, width), jnp.bfloat16)
        .at[recv_slot]
        .set(arrived.reshape(-1, width), mode="drop")
    )
    starts_flag = jnp.concatenate(
        [jnp.ones((1,), jnp.int32), (slot_ids[1:] != slot_ids[:-1]).astype(jnp.int32)]
    )
    segment = jnp.cumsum(starts_flag)
    section_idx = lax.axis_index("section")
    params = (
        pre_gain[0],
        input_proj[0],
        gate_proj[0],
        state_proj[0],
        step_proj[0],
        step_bias[0],
        decay_log[0],
        skip_gain[0],
        norm_gain[0],
        out_proj[0],
    )
    local_heads = step_proj.shape[2]
    micro_rows = own_slots // MICRO
    zero_state = (jnp.zeros((local_heads, HEADDIM, NSTATE), jnp.float32), jnp.array(-1, jnp.int32))
    cot_own = cotangent[0]
    carried_state = zero_state
    handed = jnp.zeros((micro_rows, feat_width), jnp.bfloat16)
    outputs_all = jnp.zeros((own_slots, feat_width), jnp.bfloat16)
    grad_acc = jnp.zeros((out_proj.shape[1], feat_width), jnp.float32)
    for turn_index in range(MICRO + 1):
        micro_index = turn_index - section_idx
        active_turn = (micro_index >= 0) & (micro_index < MICRO)
        micro_index = jnp.clip(micro_index, 0, MICRO - 1)
        first_row = micro_index * micro_rows
        own_in = lax.dynamic_slice_in_dim(stream, first_row, micro_rows, 0)
        source = jnp.where(section_idx == 0, own_in, handed)
        seg_part = lax.dynamic_slice_in_dim(segment, first_row, micro_rows, 0)
        result, y_norm, moved = block_layer(source, seg_part, carried_state, params)
        carried_state = jax.tree.map(
            lambda new_val, old_val: jnp.where(active_turn, new_val, old_val), moved, carried_state
        )
        outputs_all = jnp.where(
            active_turn,
            lax.dynamic_update_slice_in_dim(outputs_all, result, first_row, 0),
            outputs_all,
        )
        cot_part = lax.dynamic_slice_in_dim(cot_own, first_row, micro_rows, 0)
        grad_acc = grad_acc + jnp.where(active_turn, grad_term(y_norm, cot_part), 0.0)
        if turn_index < MICRO:
            handed = from_behind(result, "section", 1)
    grad_share = lax.psum_scatter(
        grad_acc.astype(jnp.bfloat16), "dp", scatter_dimension=1, tiled=True
    )
    return (outputs_all[None], grad_share[None])


def solution(mesh):
    return jax.shard_map(
        per_device,
        mesh=mesh,
        in_specs=(
            P("dp", None),
            P(),
            P(),
            P("section", "dp", None),
            P("section", None),
            P("section", None, "tensor"),
            P("section", None, "tensor"),
            P("section", None, None),
            P("section", None, "tensor"),
            P("section", "tensor"),
            P("section", "tensor"),
            P("section", "tensor"),
            P("section", "tensor"),
            P("section", "tensor", None),
        ),
        out_specs=(P("section", "dp", None), P("section", "tensor", "dp")),
        check_vma=False,
    )
```

profile of v0, /device:TPU:1, one launch (start us, length us, event | category | flops | bytes accessed | tf_op | source)
XLA Modules:
  0.0 641.2 jit_solution(3707332609720669846)
XLA Ops:
  7.2 1.0 select_reduce_fusion.3
  10.8 4.4 scatter_custom_fusion
  15.2 12.3 %all-to-all-start = ((bf16[32,16,2048]{2,1,0:T(8,128)(2,1)}), bf16[32,16,2048]{2,1,0:T(8,128)(2,1)}, u32[]{:S(2)}, u32[]{:S(2)}) async-start(bf16[32,16,2048]{2,1,0:T(8,128)(2,1)} %bitcast.297), calls=%async_computation | async-start | bytes 4194304 | tf_op jit(solution)/shard_map/all_to_all | solution.py:205
  28.8 2.4 scatter_custom_fusion.2
  32.7 43.2 %all-to-all-done = bf16[32,16,2048]{2,1,0:T(8,128)(2,1)} async-done(((bf16[32,16,2048]{2,1,0:T(8,128)(2,1)}), bf16[32,16,2048]{2,1,0:T(8,128)(2,1)}, u32[]{:S(2)}, u32[]{:S(2)}) %all-to-all-start) | async-done | bytes 2097184 | tf_op jit(solution)/shard_map/all_to_all | solution.py:205
  76.0 6.1 scatter_custom_fusion.1
  82.1 1.6 multiply_reduce_fusion.2
  83.7 1.7 compare_select_fusion.2
  86.2 2.2 multiply_convert_fusion.20
  90.2 1.1 broadcast.415.clone2
  91.3 33.7 %while.45 = (s32[]{:T(128)}, f32[8,64,128]{2,1,0:T(8,128)S(1)}, s32[]{:T(128)}, f32[4,64,8,64]{3,2,1,0:T(8,128)}, s32[4,64]{1,0:T(4,128)S(1)}, /*index=5*/f32[4,...) while((s32[]{:T(128)}, f32[8,64,128]{2,1,0:T(8,128)S(1)}, ...), condition=%wide.region_17.18_spmd.clone, body=%wide.region_15.17_spmd.clone.sunk | while | flops 22689996 | bytes 2389582 | solution.py:78
  97.4 0.9 convolution_add_fusion.11
  105.9 0.9 convolution_add_fusion.11
  114.3 0.9 convolution_add_fusion.11
  125.0 1.5 reshape.687
  126.5 2.9 multiply_reduce_fusion.5
  129.4 8.8 %psum.21 = f32[256]{0:T(256)S(1)} all-reduce(f32[256]{0:T(256)S(1)} %get-tuple-element.392), channel_id=1, replica_groups=mesh['dp'=32,'section'=2,'tensor'=4] {'tensor'}, use_global_device_ids=true, to_apply=%region_19.20 | all-reduce | flops 256 | bytes 2048 | tf_op jit(solution)/shard_map/psum | solution.py:126
  138.2 3.3 convolution_convert_fusion.2
  141.7 2.8 fusion.116
  144.5 20.9 %reduce-scatter.5.cloned.1.call-done = bf16[64,2048]{1,0:T(8,128)(2,1)} async-done(((bf16[256,2048]{1,0:T(8,128)(2,1)}), bf16[64,2048]{1,0:T(8,128)(2,1)}) %reduce-scatter.5.cloned.1.call-update) | async-done | bytes 262160 | tf_op jit(solution)/shard_map/reduce_scatter | solution.py:131
  165.4 1.9 add_convert_fusion.3
  167.4 26.8 %all-gather.4.cloned.1.call-done = bf16[256,2048]{1,0:T(8,128)(2,1)} async-done(((bf16[64,2048]{1,0:T(8,128)(2,1)}), bf16[256,2048]{1,0:T(8,128)(2,1)}) %all-gather.4.cloned.1.call-update) | async-done | bytes 1048592 | tf_op jit(solution)/shard_map/all_gather | solution.py:139
  194.1 1.3 collective-permute-start
  196.2 3.3 collective-permute-done
  199.5 3.3 fusion.154
  205.0 1.0 copy-done.28
  207.0 1.1 reshape_reshape.10
  208.1 1.0 broadcast.415.clone2.1
  209.1 30.9 %while.43 = (s32[]{:T(128)}, f32[8,64,128]{2,1,0:T(8,128)S(1)}, s32[]{:T(128)}, f32[4,64,8,64]{3,2,1,0:T(8,128)}, s32[4,64]{1,0:T(4,128)}, /*index=5*/f32[4,64,8...) while((s32[]{:T(128)}, f32[8,64,128]{2,1,0:T(8,128)S(1)}, ...), condition=%wide.region_24.25_spmd, body=%wide.region_22.24_spmd.sunk | while | flops 22624460 | bytes 2581539 | solution.py:78
  212.9 0.9 constant_dynamic-slice_fusion.12
  220.6 0.9 constant_dynamic-slice_fusion.12
  228.4 0.9 constant_dynamic-slice_fusion.12
  236.1 0.9 constant_dynamic-slice_fusion.12
  240.0 2.3 reshape.692
  242.3 3.0 multiply_reduce_fusion.4
  245.4 7.5 %psum.22 = f32[256]{0:T(256)S(1)} all-reduce(f32[256]{0:T(256)S(1)} %get-tuple-element.394), channel_id=1, replica_groups=mesh['dp'=32,'section'=2,'tensor'=4] {'tensor'}, use_global_device_ids=true, to_apply=%region_26.27 | all-reduce | flops 256 | bytes 2048 | tf_op jit(solution)/shard_map/psum | solution.py:126
  252.9 3.3 convolution_convert_fusion.1
  256.3 25.2 %reduce-scatter.7.cloned.1.call-done = bf16[64,2048]{1,0:T(8,128)(2,1)} async-done(((bf16[256,2048]{1,0:T(8,128)(2,1)}), bf16[64,2048]{1,0:T(8,128)(2,1)}) %reduce-scatter.7.cloned.1.call-update) | async-done | bytes 262160 | tf_op jit(solution)/shard_map/reduce_scatter | solution.py:131
  281.5 1.9 add_convert_fusion.2
  283.4 26.8 %all-gather.6.cloned.1.call-done = bf16[256,2048]{1,0:T(8,128)(2,1)} async-done(((bf16[64,2048]{1,0:T(8,128)(2,1)}), bf16[256,2048]{1,0:T(8,128)(2,1)}) %all-gather.6.cloned.1.call-update) | async-done | bytes 1048592 | tf_op jit(solution)/shard_map/all_gather | solution.py:139
  310.2 1.5 collective-permute-start.1
  311.9 3.7 collective-permute-done.1
  315.6 3.3 fusion.153
  321.1 1.0 copy-done.29
  323.1 1.1 reshape_reshape.11
  324.2 1.0 broadcast.415.clone
  325.2 22.8 %while.44 = (s32[]{:T(128)}, f32[8,64,128]{2,1,0:T(8,128)S(1)}, s32[]{:T(128)}, f32[4,64,8,64]{3,2,1,0:T(8,128)}, s32[4,64]{1,0:T(4,128)S(1)}, /*index=5*/f32[4,...) while((s32[]{:T(128)}, f32[8,64,128]{2,1,0:T(8,128)S(1)}, ...), condition=%wide.region_31.32_spmd, body=%wide.region_29.31_spmd.sunk | while | flops 22624460 | bytes 2582019 | solution.py:78
  327.7 0.9 constant_dynamic-slice_fusion.13
  333.3 0.9 constant_dynamic-slice_fusion.13
  339.0 0.9 constant_dynamic-slice_fusion.13
  344.7 0.9 constant_dynamic-slice_fusion.13
  348.0 1.5 reshape.697
  349.5 2.9 multiply_reduce_fusion.3
  352.4 7.5 %psum.23 = f32[256]{0:T(256)S(1)} all-reduce(f32[256]{0:T(256)S(1)} %get-tuple-element.396), channel_id=1, replica_groups=mesh['dp'=32,'section'=2,'tensor'=4] {'tensor'}, use_global_device_ids=true, to_apply=%region_33.34 | all-reduce | flops 256 | bytes 2048 | tf_op jit(solution)/shard_map/psum | solution.py:126
  359.9 3.3 convolution_convert_fusion
  363.3 25.1 %reduce-scatter.9.cloned.1.call-done = bf16[64,2048]{1,0:T(8,128)(2,1)} async-done(((bf16[256,2048]{1,0:T(8,128)(2,1)}), bf16[64,2048]{1,0:T(8,128)(2,1)}) %reduce-scatter.9.cloned.1.call-update) | async-done | bytes 262160 | tf_op jit(solution)/shard_map/reduce_scatter | solution.py:131
  388.4 1.9 add_convert_fusion.1
  392.3 2.5 add_convert_fusion
  395.0 0.9 copy-done.10
  396.7 1.3 copy-done.1
  398.0 1.3 copy.198
  399.3 17.9 %all-gather.8.cloned.1.call-done = bf16[256,2048]{1,0:T(8,128)(2,1)} async-done(((bf16[64,2048]{1,0:T(8,128)(2,1)}), bf16[256,2048]{1,0:T(8,128)(2,1)}) %all-gather.8.cloned.1.call-update) | async-done | bytes 1048592 | tf_op jit(solution)/shard_map/all_gather | solution.py:139
  417.2 2.9 bitcast_dynamic-update-slice_fusion
  420.1 214.3 %reduce-scatter.11.cloned.1.call-done = bf16[512,64]{0,1:T(8,128)(2,1)} async-done(((bf16[512,2048]{0,1:T(8,128)(2,1)}), bf16[512,64]{0,1:T(8,128)(2,1)}) %reduce-scatter.11.cloned.1.call-update) | async-done | bytes 65552 | tf_op jit(solution)/shard_map/reduce_scatter | solution.py:258
  (407 shorter events, 79.5 us)
Async XLA Ops:
  7.2 383.2 %copy-start = (bf16[1,512,2048]{2,1,0:T(8,128)(2,1)S(1)}, bf16[1,512,2048]{2,1,0:T(8,128)(2,1)}, u32[]{:S(2)}) copy-start(bf16[1,512,2048]{2,1,0:T(8,128)(2,1)} %param.23) | copy-start | bytes 6291460
  15.2 12.4 %copy-start.26 = (f32[1,8]{1,0:T(1,128)S(1)}, f32[1,8]{1,0:T(1,128)}, u32[]{:S(2)}) copy-start(f32[1,8]{1,0:T(1,128)} %param.31) | copy-start | bytes 100
  15.2 13.2 %copy-start.20 = (s32[128]{0:T(128)S(1)}, s32[128]{0:T(128)}, u32[]{:S(2)}) copy-start(s32[128]{0:T(128)} %param.22) | copy-start | bytes 1540
  15.2 13.2 %copy-start.19 = (s32[128]{0:T(128)S(1)}, s32[128]{0:T(128)}, u32[]{:S(2)}) copy-start(s32[128]{0:T(128)} %param.21) | copy-start | bytes 1540
  15.2 17.5 %copy-start.38 = (f32[1,8]{1,0:T(1,128)S(1)}, f32[1,8]{1,0:T(1,128)}, u32[]{:S(2)}) copy-start(f32[1,8]{1,0:T(1,128)} %param.30) | copy-start | bytes 100
  15.2 60.8 %all-to-all-start = ((bf16[32,16,2048]{2,1,0:T(8,128)(2,1)}), bf16[32,16,2048]{2,1,0:T(8,128)(2,1)}, u32[]{:S(2)}, u32[]{:S(2)}) async-start(bf16[32,16,2048]{2,1,0:T(8,128)(2,1)} %bitcast.297), calls=%async_computation | async-start | bytes 4194304 | tf_op jit(solution)/shard_map/all_to_all | solution.py:205
  27.5 56.2 %copy-start.32 = (bf16[1,2048,8]{1,2,0:T(8,128)(2,1)S(1)}, bf16[1,2048,8]{1,2,0:T(8,128)(2,1)}, u32[]{:S(2)}) copy-start(bf16[1,2048,8]{1,2,0:T(8,128)(2,1)} %param.28) | copy-start | bytes 98308
  27.5 56.2 %copy-start.35 = (f32[1,2048]{1,0:T(1,128)S(1)}, f32[1,2048]{1,0:T(1,128)}, u32[]{:S(2)}) copy-start(f32[1,2048]{1,0:T(1,128)} %param.24) | copy-start | bytes 24580
  27.5 56.2 %copy-start.39 = (f32[1,8]{1,0:T(1,128)S(1)}, f32[1,8]{1,0:T(1,128)}, u32[]{:S(2)}) copy-start(f32[1,8]{1,0:T(1,128)} %param.29) | copy-start | bytes 100
  27.5 137.9 %reduce-scatter.5.cloned.1.call-start = ((), (), s32[]{:S(2)}) async-start(), calls=%async_computation.5 | async-start | bytes 1310720 | tf_op jit(solution)/shard_map/reduce_scatter | solution.py:131
  83.7 5.4 copy-start.24
  86.2 2.9 copy-start.2
  86.2 2.9 copy-start.27
  89.9 1.4 copy-start.14
  91.3 4.2 copy-start.17
  96.4 2.7 copy-start.18
  99.7 4.3 copy-start.17
  104.8 2.7 copy-start.18
  108.1 4.3 copy-start.17
  113.2 2.7 copy-start.18
  116.6 4.3 copy-start.17
  121.7 2.7 copy-start.18
  126.5 11.7 %copy-start.11 = (f32[1,512]{1,0:T(1,128)S(1)}, f32[1,512]{1,0:T(1,128)}, u32[]{:S(2)}) copy-start(f32[1,512]{1,0:T(1,128)} %param.32) | copy-start | bytes 6148
  129.4 12.2 %copy-start.5 = (f32[256,512]{1,0:T(8,128)}, f32[256,512]{1,0:T(8,128)S(1)}, u32[]{:S(2)}) copy-start(f32[256,512]{1,0:T(8,128)S(1)} %get-tuple-element.393) | copy-start | bytes 1572868
  138.2 3.4 copy-start.15
  141.6 52.5 %all-gather.4.cloned.1.call-start = ((), (), s32[]{:S(2)}) async-start(), calls=%async_computation.6 | async-start | bytes 1310720 | tf_op jit(solution)/shard_map/all_gather | solution.py:139
  141.7 53.8 %copy-start.22 = (s32[256]{0:T(256)S(1)}, s32[256]{0:T(256)}, u32[]{:S(2)}) copy-start(s32[256]{0:T(256)} %get-tuple-element.388) | copy-start | bytes 3076
  167.3 114.2 %reduce-scatter.7.cloned.1.call-start = ((), (), s32[]{:S(2)}) async-start(), calls=%async_computation.7 | async-start | bytes 1310720 | tf_op jit(solution)/shard_map/reduce_scatter | solution.py:131
  194.1 5.3 collective-permute-start
  196.1 7.0 %copy-start.33 = (bf16[1,2048,8]{1,2,0:T(8,128)(2,1)S(1)}, bf16[1,2048,8]{1,2,0:T(8,128)(2,1)}, u32[]{:S(2)}) copy-start(bf16[1,2048,8]{1,2,0:T(8,128)(2,1)} %param.28) | copy-start | bytes 98308
  196.1 7.0 %copy-start.36 = (f32[1,2048]{1,0:T(1,128)S(1)}, f32[1,2048]{1,0:T(1,128)}, u32[]{:S(2)}) copy-start(f32[1,2048]{1,0:T(1,128)} %param.24) | copy-start | bytes 24580
  196.2 7.0 %copy-start.40 = (f32[1,8]{1,0:T(1,128)S(1)}, f32[1,8]{1,0:T(1,128)}, u32[]{:S(2)}) copy-start(f32[1,8]{1,0:T(1,128)} %param.29) | copy-start | bytes 100
  202.8 2.1 copy-start.4
  202.8 1.6 copy-start.30
  203.1 1.8 copy-start.25
  204.4 1.6 copy-start.28
  206.8 2.3 copy-start.13
  245.4 10.9 %copy-start.7 = (f32[256,512]{1,0:T(8,128)}, f32[256,512]{1,0:T(8,128)S(1)}, u32[]{:S(2)}) copy-start(f32[256,512]{1,0:T(8,128)S(1)} %get-tuple-element.395) | copy-start | bytes 1572868
  256.2 55.5 %copy-start.21 = (s32[256]{0:T(256)S(1)}, s32[256]{0:T(256)}, u32[]{:S(2)}) copy-start(s32[256]{0:T(256)} %get-tuple-element.387) | copy-start | bytes 3076
  256.3 53.9 %all-gather.6.cloned.1.call-start = ((), (), s32[]{:S(2)}) async-start(), calls=%async_computation.8 | async-start | bytes 1310720 | tf_op jit(solution)/shard_map/all_gather | solution.py:139
  283.4 105.0 %reduce-scatter.9.cloned.1.call-start = ((), (), s32[]{:S(2)}) async-start(), calls=%async_computation.9 | async-start | bytes 1310720 | tf_op jit(solution)/shard_map/reduce_scatter | solution.py:131
  310.2 5.3 collective-permute-start.1
  311.9 7.3 %copy-start.34 = (bf16[1,2048,8]{1,2,0:T(8,128)(2,1)S(1)}, bf16[1,2048,8]{1,2,0:T(8,128)(2,1)}, u32[]{:S(2)}) copy-start(bf16[1,2048,8]{1,2,0:T(8,128)(2,1)} %param.28) | copy-start | bytes 98308
  311.9 7.3 %copy-start.37 = (f32[1,2048]{1,0:T(1,128)S(1)}, f32[1,2048]{1,0:T(1,128)}, u32[]{:S(2)}) copy-start(f32[1,2048]{1,0:T(1,128)} %param.24) | copy-start | bytes 24580
  311.9 7.3 %copy-start.41 = (f32[1,8]{1,0:T(1,128)S(1)}, f32[1,8]{1,0:T(1,128)}, u32[]{:S(2)}) copy-start(f32[1,8]{1,0:T(1,128)} %param.29) | copy-start | bytes 100
  318.9 2.2 copy-start.3
  318.9 1.6 copy-start.31
  320.5 1.6 copy-start.29
  322.9 2.3 copy-start.12
  325.2 24.3 %copy-start.23 = (f32[512]{0:T(512)S(1)}, f32[512]{0:T(512)}, u32[]{:S(2)}) copy-start(f32[512]{0:T(512)} %mul.547) | copy-start | bytes 6148
  363.2 27.2 %copy-start.6 = (f32[256,512]{1,0:T(8,128)S(1)}, f32[256,512]{1,0:T(8,128)}, u32[]{:S(2)}) copy-start(f32[256,512]{1,0:T(8,128)} %copy-done.5) | copy-start | bytes 1572868
  363.2 27.2 %copy-start.16 = (f32[256]{0:T(256)S(1)}, f32[256]{0:T(256)}, u32[]{:S(2)}) copy-start(f32[256]{0:T(256)} %copy-done.15) | copy-start | bytes 3076
  363.2 54.0 %all-gather.8.cloned.1.call-start = ((), (), s32[]{:S(2)}) async-start(), calls=%async_computation.10 | async-start | bytes 1310720 | tf_op jit(solution)/shard_map/all_gather | solution.py:139
  390.3 244.0 %reduce-scatter.11.cloned.1.call-start = ((), (), s32[]{:S(2)}) async-start(), calls=%async_computation.11 | async-start | bytes 2162688 | tf_op jit(solution)/shard_map/reduce_scatter | solution.py:258
  390.4 1.0 copy-start.8
  394.7 1.2 copy-start.10
  394.8 1.5 copy-start.9
  396.7 1.3 copy-start.1
Sparse Core Ops, SparseCore 0:
  141.7 23.6 reduce-scatter.4
  167.4 26.6 all-gather.3
  256.4 25.0 reduce-scatter.6
  283.5 26.6 all-gather.5
  363.3 25.0 reduce-scatter.8
  390.4 26.6 all-gather.7
  422.1 212.2 reduce-scatter.10
where the time goes:
time: 648 us; the launch traced here: 641 us
  waiting for transfers between devices  407 us (63%)
  local copies, waits for them, and re-layouts  66.8 us (10%)
  matrix products  51.8 us (8%)
  other arithmetic  45.6 us (7%)
  blocking collectives  23.8 us (4%)
  loops' own time  15.7 us (2%)
  starting transfers between devices  15.4 us (2%)
  between operations  14.8 us (2%)
    reduce_scatter x1, waiting for transfers between devices, per_device(): lax.psum_scatter(grad_acc.astype(jnp.bfloat16), 'dp', scatter_dimension=1...  214 us
    all_gather x3, waiting for transfers between devices, block_layer(): result = lax.all_gather(own_out, 'tensor', axis=0, tiled=True)  71.5 us
    reduce_scatter x3, waiting for transfers between devices, block_layer(): lax.psum_scatter(jnp.dot(y_norm, out_proj, preferred_element_type=jnp.flo...  71.2 us
    all_to_all x1, waiting for transfers between devices, per_device(): lax.all_to_all(outgoing, 'dp', split_axis=0, concat_axis=0, tiled=True)  43.2 us
    psum x3, blocking collectives, block_layer(): sq_sum = lax.psum(jnp.sum(gated * gated, axis=-1), 'tensor')  23.8 us
    another operation x3, loops' own time, block_scan(): lax.scan(advance, (state, prev_segment), scanned)  15.7 us
  transfers between devices with their start and end apart: 10, of which 10 were waited for; matrix products, arithmetic and copies ran while one was open for 3% of the time, Pallas kernels for 0%

commit v1 on v0

v1 whole, which is shorter than its diff:
```python
import functools

import jax
import jax.numpy as jnp
from jax import lax
from jax.experimental import pallas as pl
from jax.experimental.pallas import tpu as pltpu
from jax.sharding import PartitionSpec as P

MESH = pl.DeviceIdType.MESH
HEADDIM = 64
NSTATE = 128
ROWS = 128
RING = 4
EPS = 1e-05
F32 = jnp.float32
BF16 = jnp.bfloat16


def layout_tables(base_rows, baseline_owner):
    count = base_rows.shape[0]
    index = jnp.arange(count, dtype=jnp.int32)
    ends = jnp.cumsum(base_rows)
    starts = ends - base_rows
    earlier = (baseline_owner[:, None] == baseline_owner[None, :]) & (
        index[None, :] < index[:, None]
    )
    owner_start = jnp.sum(jnp.where(earlier, base_rows[None, :], 0), axis=1)
    return (index, starts, ends, owner_start)


def iota(shape, axis):
    return lax.broadcasted_iota(jnp.int32, shape, axis)


def silu(value):
    return value / (1.0 + jnp.exp(-value))


def softplus(value):
    return jnp.maximum(value, 0.0) + jnp.log1p(jnp.exp(-jnp.abs(value)))


def owner_starts(rows_c, rows_r, own_c, own_r):
    count = rows_r.shape[1]
    down, across = iota((count, count), 0), iota((count, count), 1)
    same = own_c == own_r
    row = jnp.sum(jnp.where(same & (down < across), rows_c, 0), axis=0, keepdims=True)
    col = jnp.sum(jnp.where(same & (across < down), rows_r, 0), axis=1, keepdims=True)
    return row, col


def block_kernel(
    chunks,
    heads,
    rows_c,
    rows_r,
    own_c,
    own_r,
    stream,
    pre_gain,
    w_in,
    w_gate,
    w_state,
    w_step,
    step_bias,
    decay_log,
    skip_gain,
    norm_gain,
    w_out,
    out_ref,
    y_ref,
    rs_ref,
    u_buf,
    o_buf,
    p_buf,
    a1,
    b1,
    a2,
    b2,
    normed,
    xs_buf,
    gate_buf,
    bc_buf,
    dt_buf,
    state,
    prev,
    seg_col,
    seg_row,
    sq_buf,
    skip_row,
    hand_sem,
    hand_send,
    out_sem,
    rs_send,
    rs_recv,
    ag_send,
    ag_recv,
    sq_send,
    sq_recv,
):
    me = lax.axis_index("tensor")
    sec = lax.axis_index("section")
    owner = lax.axis_index("dp")
    right, left, opposite = ((me + 1) % RING, (me + 3) % RING, (me + 2) % RING)
    width = o_buf.shape[1]
    readers = lax.axis_size("dp")
    inner = w_in.shape[1]
    pairs = heads // 2
    piece = ROWS // RING
    half = piece // 2
    count = rows_r.shape[1]

    barrier = pltpu.get_barrier_semaphore()
    for other in (right, left, opposite):
        pl.semaphore_signal(barrier, inc=1, device_id={"tensor": other}, device_id_type=MESH)
    pl.semaphore_signal(barrier, inc=1, device_id={"section": 1 - sec}, device_id_type=MESH)

    def rows_of(t):
        return pl.ds(pl.multiple_of(t * ROWS, ROWS), ROWS)

    def piece_of(who, which=None):
        if which is None:
            return pl.ds(pl.multiple_of(who * piece, piece), piece)
        return pl.ds(pl.multiple_of(who * piece + which * half, half), half)

    def out_piece(t, who, which=None):
        if which is None:
            return pl.ds(pl.multiple_of(t * ROWS + who * piece, piece), piece)
        return pl.ds(pl.multiple_of(t * ROWS + who * piece + which * half, half), half)

    def push(src, dst, send_sem, recv_sem, who):
        return pltpu.make_async_remote_copy(
            src_ref=src,
            dst_ref=dst,
            send_sem=send_sem,
            recv_sem=recv_sem,
            device_id={"tensor": who},
            device_id_type=MESH,
        )

    def feed(t):
        return pltpu.make_async_copy(stream.at[rows_of(t)], u_buf.at[rows_of(t)], hand_sem.at[t])

    def hand_over(t):
        return pltpu.make_async_remote_copy(
            src_ref=o_buf.at[rows_of(t)],
            dst_ref=u_buf.at[rows_of(t)],
            send_sem=hand_send.at[t],
            recv_sem=hand_sem.at[t],
            device_id={"section": 1 - sec},
            device_id_type=MESH,
        )

    def store_out(t):
        return pltpu.make_async_copy(o_buf.at[rows_of(t)], out_ref.at[rows_of(t)], out_sem.at[t])

    @pl.when(sec == 0)
    def _():
        for t in range(chunks):
            feed(t).start()

    start_row, start_col = owner_starts(rows_c[...], rows_r[...], own_c[...], own_r[...])
    slots = chunks * ROWS
    ids_c = (iota((count, 1), 0) + 1).astype(F32)
    ids_r = (iota((1, count), 1) + 1).astype(F32)
    slot_r = iota((count, slots), 1)
    held_c = (
        (own_c[...] == owner)
        & (slot_r >= readers * start_col)
        & (slot_r < readers * (start_col + rows_c[...]))
    )
    ids_row = jnp.sum(jnp.where(held_c, ids_c, 0.0), axis=0, keepdims=True)
    for t in range(chunks):
        seg_row[t] = jnp.broadcast_to(ids_row[:, t * ROWS : (t + 1) * ROWS], (8, ROWS))
    slot_c = iota((slots, count), 0)
    held_r = (
        (own_r[...] == owner)
        & (slot_c >= readers * start_row)
        & (slot_c < readers * (start_row + rows_r[...]))
    )
    ids_col = jnp.sum(jnp.where(held_r, ids_r, 0.0), axis=1, keepdims=True)
    seg_col[...] = jnp.broadcast_to(ids_col, (slots, ROWS))
    state[...] = jnp.zeros_like(state)
    prev[...] = jnp.full(prev.shape, -1.0, F32)
    lane = iota((ROWS, 128), 1)
    low = lane < HEADDIM

    def spread(value, pair):
        shape = (value.shape[0], 128)
        first = jnp.broadcast_to(value[:, 2 * pair : 2 * pair + 1], shape)
        second = jnp.broadcast_to(value[:, 2 * pair + 1 : 2 * pair + 2], shape)
        return jnp.where(iota(shape, 1) < HEADDIM, first, second)

    for pair in range(pairs):
        skip_row[:, pair * 128 : (pair + 1) * 128] = spread(
            jnp.broadcast_to(skip_gain[...], (8, 128)), pair
        )
    rate = -jnp.exp(decay_log[...])
    pl.semaphore_wait(barrier, 4)

    def stage_in(t):
        pltpu.make_async_copy(u_buf.at[rows_of(t)], u_buf.at[rows_of(t)], hand_sem.at[t]).wait()
        rows_f = u_buf[rows_of(t), :].astype(F32)
        scale = lax.rsqrt(jnp.mean(rows_f * rows_f, axis=-1, keepdims=True) + EPS)
        normed[...] = (rows_f * scale * pre_gain[...]).astype(BF16)
        xs_buf[...] = silu(jnp.dot(normed[...], w_in[...], preferred_element_type=F32)).astype(BF16)
        bc_buf[...] = silu(jnp.dot(normed[...], w_state[...], preferred_element_type=F32)).astype(
            BF16
        )
        dt_buf[...] = softplus(
            jnp.dot(normed[...], w_step[...], preferred_element_type=F32) + step_bias[...]
        )
        gate_buf[...] = silu(jnp.dot(normed[...], w_gate[...], preferred_element_type=F32))

    def stage_scan(t):
        segment_c = seg_col[rows_of(t), :]
        segment_r = jnp.broadcast_to(seg_row[t][0:1, :], (ROWS, ROWS))
        before = jnp.broadcast_to(prev[0:1, :], (ROWS, ROWS))
        last = segment_c[ROWS - 1 : ROWS, :]
        down, across = iota((ROWS, ROWS), 0), iota((ROWS, ROWS), 1)
        causal = down >= across
        hidden = jnp.where(causal & (segment_c == segment_r), 0.0, -1e30)
        dt = dt_buf[...]
        cum = jnp.dot(
            causal.astype(F32),
            dt * rate,
            preferred_element_type=F32,
            precision=lax.Precision.HIGHEST,
        )
        cum_t, dt_t = cum.T, dt.T
        grown = jnp.exp(cum)
        from_before = jnp.where(segment_c == before, grown, 0.0)
        last_cum = cum[ROWS - 1 : ROWS, :]
        tail = jnp.where(segment_c == last, jnp.exp(last_cum - cum), 0.0) * dt
        kept = jnp.where(last == prev[0:1, :], jnp.exp(last_cum), 0.0)
        b_rows, c_rows = bc_buf[:, :NSTATE], bc_buf[:, NSTATE:]
        scores = lax.dot_general(
            c_rows, b_rows, (((1,), (1,)), ((), ())), preferred_element_type=F32
        )
        readout = jnp.dot(c_rows, state[...].astype(BF16), preferred_element_type=F32)
        squares = jnp.zeros((ROWS, 128), F32)
        for pair in range(pairs):
            cols = slice(pair * 128, (pair + 1) * 128)
            x_pair = xs_buf[:, cols]
            x_f = x_pair.astype(F32)
            parts = []
            for head in (2 * pair, 2 * pair + 1):
                falling = jnp.minimum(cum[:, head : head + 1] - cum_t[head : head + 1, :], 0.0)
                weights = jnp.exp(falling + hidden) * scores * dt_t[head : head + 1, :]
                parts.append(jnp.dot(weights.astype(BF16), x_pair, preferred_element_type=F32))
            total = (
                jnp.where(low, parts[0], parts[1])
                + spread(from_before, pair) * readout[:, cols]
                + skip_row[0:1, cols] * x_f
            )
            gated = total * gate_buf[:, cols]
            squares = squares + gated * gated
            y_ref[rows_of(t), cols] = (gated * norm_gain[:, cols]).astype(BF16)
            scaled = (spread(tail, pair) * x_f).astype(BF16)
            fresh = lax.dot_general(
                b_rows, scaled, (((0,), (0,)), ((), ())), preferred_element_type=F32
            )
            state[:, cols] = spread(kept, pair) * state[:, cols] + fresh
        prev[...] = jnp.broadcast_to(last, prev.shape)
        sq_buf[0, t] = jnp.broadcast_to(jnp.sum(squares.T, axis=0, keepdims=True), (8, ROWS))

    def send_squares(t):
        return [
            push(
                sq_buf.at[0, t],
                sq_buf.at[k, t],
                sq_send.at[k - 1, t],
                sq_recv.at[k - 1, t],
                (me + k) % RING,
            )
            for k in range(1, RING)
        ]

    def reduce_copies(t):
        mine = p_buf.at[t]
        return (
            push(mine.at[piece_of(opposite, 0)], a1.at[t], rs_send.at[0, t], rs_recv.at[0, t], right),
            push(mine.at[piece_of(opposite, 1)], b1.at[t], rs_send.at[1, t], rs_recv.at[1, t], left),
            push(mine.at[piece_of(right, 1)], a2.at[t, 1], rs_send.at[2, t], rs_recv.at[2, t], right),
            push(mine.at[piece_of(left, 0)], b2.at[t, 0], rs_send.at[3, t], rs_recv.at[3, t], left),
            push(mine.at[piece_of(right, 0)], a2.at[t, 0], rs_send.at[4, t], rs_recv.at[4, t], right),
            push(mine.at[piece_of(left, 1)], b2.at[t, 1], rs_send.at[5, t], rs_recv.at[5, t], left),
        )

    def gather_copies(t):
        own, from_left, from_right = (
            o_buf.at[out_piece(t, me)],
            o_buf.at[out_piece(t, left, 0)],
            o_buf.at[out_piece(t, right, 1)],
        )
        return (
            push(own, own, ag_send.at[0, t], ag_recv.at[0, t], right),
            push(own, own, ag_send.at[1, t], ag_recv.at[1, t], left),
            push(from_left, from_left, ag_send.at[2, t], ag_recv.at[2, t], right),
            push(from_right, from_right, ag_send.at[3, t], ag_recv.at[3, t], left),
        )

    def stage_out(t):
        p_buf[t] = jnp.dot(y_ref[rows_of(t), :], w_out[...], preferred_element_type=F32).astype(
            BF16
        )
        for copy in reduce_copies(t)[:4]:
            copy.start()

    def reduce_second(t):
        copies = reduce_copies(t)
        copies[0].wait_recv()
        where = piece_of(right, 0)
        p_buf[t, where, :] = (p_buf[t, where, :].astype(F32) + a1[t].astype(F32)).astype(BF16)
        copies[4].start()
        copies[1].wait_recv()
        where = piece_of(left, 1)
        p_buf[t, where, :] = (p_buf[t, where, :].astype(F32) + b1[t].astype(F32)).astype(BF16)
        copies[5].start()

    def reduce_last(t):
        for copy in send_squares(t):
            copy.wait_recv()
        total = sq_buf[0, t] + sq_buf[1, t] + sq_buf[2, t] + sq_buf[3, t]
        scale = lax.rsqrt(total / (RING * inner) + EPS)
        rs_ref[rows_of(t), :] = jnp.broadcast_to(scale[0:1, :], (ROWS, ROWS)).T
        copies = reduce_copies(t)
        for copy in copies[2:]:
            copy.wait_recv()
        for which in (0, 1):
            where = out_piece(t, me, which)
            summed = (
                p_buf[t, piece_of(me, which), :].astype(F32)
                + a2[t, which].astype(F32)
                + b2[t, which].astype(F32)
            )
            o_buf[where, :] = (
                u_buf[where, :].astype(F32) + rs_ref[where, 0:1] * summed
            ).astype(BF16)
        for copy in gather_copies(t)[:2]:
            copy.start()

    def gather_second(t):
        copies = gather_copies(t)
        copies[0].wait_recv()
        copies[2].start()
        copies[1].wait_recv()
        copies[3].start()

    def gather_last(t):
        copies = gather_copies(t)
        copies[2].wait_recv()
        copies[3].wait_recv()

        @pl.when(sec == 0)
        def _():
            hand_over(t).start()

        store_out(t).start()

    def step(t, carry):
        @pl.when(t < chunks)
        def _():
            stage_in(t)

        @pl.when(t >= 2)
        def _():
            gather_last(t - 2)

        @pl.when((t >= 1) & (t <= chunks))
        def _():
            reduce_second(t - 1)

        @pl.when(t < chunks)
        def _():
            stage_scan(t)
            for copy in send_squares(t):
                copy.start()

        @pl.when((t >= 1) & (t <= chunks))
        def _():
            reduce_last(t - 1)

        @pl.when(t < chunks)
        def _():
            stage_out(t)

        @pl.when((t >= 1) & (t <= chunks))
        def _():
            gather_second(t - 1)

        return carry

    lax.fori_loop(0, chunks + 2, step, 0)

    def drain(t, carry):
        for copy in reduce_copies(t) + gather_copies(t) + tuple(send_squares(t)):
            copy.wait_send()

        @pl.when(sec == 0)
        def _():
            hand_over(t).wait_send()

        store_out(t).wait()
        return carry

    lax.fori_loop(0, chunks, drain, 0)


def run_blocks(tables, stream, params):
    (
        pre_gain,
        input_proj,
        gate_proj,
        state_proj,
        step_proj,
        step_bias,
        decay_log,
        skip_gain,
        norm_gain,
        out_proj,
    ) = params
    slots, width = stream.shape
    inner = input_proj.shape[1]
    heads = step_proj.shape[1]
    chunks = slots // ROWS
    pad = ((0, 0), (0, 128 - heads))
    vmem = pl.BlockSpec(memory_space=pltpu.VMEM)
    anywhere = pl.BlockSpec(memory_space=pl.ANY)
    piece = ROWS // RING
    half = piece // 2
    dma = pltpu.SemaphoreType.DMA
    return pl.pallas_call(
        functools.partial(block_kernel, chunks, heads),
        name="blocks",
        out_shape=(
            jax.ShapeDtypeStruct((slots, width), BF16),
            jax.ShapeDtypeStruct((slots, inner), BF16),
            jax.ShapeDtypeStruct((slots, 128), F32),
        ),
        in_specs=[vmem] * 4 + [anywhere] + [vmem] * 10,
        out_specs=(anywhere, vmem, vmem),
        scratch_shapes=[
            pltpu.VMEM((slots, width), BF16),
            pltpu.VMEM((slots, width), BF16),
            pltpu.VMEM((chunks, ROWS, width), BF16),
            pltpu.VMEM((chunks, half, width), BF16),
            pltpu.VMEM((chunks, half, width), BF16),
            pltpu.VMEM((chunks, 2, half, width), BF16),
            pltpu.VMEM((chunks, 2, half, width), BF16),
            pltpu.VMEM((ROWS, width), BF16),
            pltpu.VMEM((ROWS, inner), BF16),
            pltpu.VMEM((ROWS, inner), F32),
            pltpu.VMEM((ROWS, 2 * NSTATE), BF16),
            pltpu.VMEM((ROWS, 128), F32),
            pltpu.VMEM((NSTATE, inner), F32),
            pltpu.VMEM((8, 128), F32),
            pltpu.VMEM((slots, 128), F32),
            pltpu.VMEM((chunks, 8, 128), F32),
            pltpu.VMEM((RING, chunks, 8, 128), F32),
            pltpu.VMEM((8, inner), F32),
            dma((chunks,)),
            dma((chunks,)),
            dma((chunks,)),
            dma((6, chunks)),
            dma((6, chunks)),
            dma((4, chunks)),
            dma((4, chunks)),
            dma((3, chunks)),
            dma((3, chunks)),
        ],
        compiler_params=pltpu.CompilerParams(
            collective_id=1, has_side_effects=True, vmem_limit_bytes=60 * 1024 * 1024
        ),
    )(
        *tables,
        stream,
        pre_gain[None],
        input_proj,
        gate_proj,
        state_proj,
        jnp.pad(step_proj, pad),
        jnp.pad(step_bias[None], pad),
        jnp.pad(decay_log[None], pad),
        jnp.pad(skip_gain[None], pad),
        norm_gain[None],
        out_proj,
    )


def grad_kernel(
    y_ref,
    rs_ref,
    cot,
    out_ref,
    yn,
    g_buf,
    a1,
    b1,
    a2,
    b2,
    h_buf,
    z_buf,
    rs_send,
    rs_recv,
    z_send,
    z_recv,
):
    levels, share = g_buf.shape[0], g_buf.shape[2]
    index = lax.axis_index("dp")
    my_z, my_y = index // RING, index % RING
    right_y, left_y, opposite_y = ((my_y + 1) % RING, (my_y + 3) % RING, (my_y + 2) % RING)
    right, left = my_z * RING + right_y, my_z * RING + left_y
    block = RING * share
    some = levels // 2

    def level(k):
        return ((my_z + k) % levels) * RING + my_y

    barrier = pltpu.get_barrier_semaphore()
    others = [right, left] + [level(k) for k in range(1, levels)]
    for other in others:
        pl.semaphore_signal(barrier, inc=1, device_id={"dp": other}, device_id_type=MESH)

    yn[...] = (y_ref[...].astype(F32) * rs_ref[:, 0:1]).astype(BF16)

    def push(src, dst, send_sem, recv_sem, who):
        return pltpu.make_async_remote_copy(
            src_ref=src,
            dst_ref=dst,
            send_sem=send_sem,
            recv_sem=recv_sem,
            device_id={"dp": who},
            device_id_type=MESH,
        )

    low, high = pl.ds(0, some), pl.ds(some, some)
    copies = (
        push(g_buf.at[low, opposite_y], a1, rs_send.at[0], rs_recv.at[0], right),
        push(g_buf.at[high, opposite_y], b1, rs_send.at[1], rs_recv.at[1], left),
        push(g_buf.at[high, right_y], a2.at[high], rs_send.at[2], rs_recv.at[2], right),
        push(g_buf.at[low, left_y], b2.at[low], rs_send.at[3], rs_recv.at[3], left),
        push(g_buf.at[low, right_y], a2.at[low], rs_send.at[4], rs_recv.at[4], right),
        push(g_buf.at[high, left_y], b2.at[high], rs_send.at[5], rs_recv.at[5], left),
    )

    def term(k, carry):
        cols = pl.ds(pl.multiple_of(k * block, block), block)
        product = lax.dot_general(
            cot[:, cols], yn[...], (((0,), (0,)), ((), ())), preferred_element_type=F32
        )
        g_buf[k] = product.astype(BF16).reshape(RING, share, product.shape[1])
        return carry

    lax.fori_loop(0, some, term, 0)
    pl.semaphore_wait(barrier, len(others))
    copies[0].start()
    copies[3].start()
    lax.fori_loop(some, levels, term, 0)
    copies[1].start()
    copies[2].start()

    copies[0].wait_recv()

    def add_low(k, carry):
        g_buf[k, right_y] = (g_buf[k, right_y].astype(F32) + a1[k].astype(F32)).astype(BF16)
        return carry

    lax.fori_loop(0, some, add_low, 0)
    copies[4].start()
    copies[1].wait_recv()

    def add_high(k, carry):
        g_buf[some + k, left_y] = (g_buf[some + k, left_y].astype(F32) + b1[k].astype(F32)).astype(
            BF16
        )
        return carry

    lax.fori_loop(0, some, add_high, 0)
    copies[5].start()
    for copy in copies[2:]:
        copy.wait_recv()

    def exchange(k):
        return push(
            h_buf.at[(my_z + k) % levels], z_buf.at[k], z_send.at[k], z_recv.at[k], level(k)
        )

    def finish(k, carry):
        who = (my_z + k) % levels
        h_buf[who] = (
            g_buf[who, my_y].astype(F32) + a2[who].astype(F32) + b2[who].astype(F32)
        ).astype(BF16)
        exchange(k).start()
        return carry

    lax.fori_loop(1, levels, finish, 0)
    total = g_buf[my_z, my_y].astype(F32) + a2[my_z].astype(F32) + b2[my_z].astype(F32)

    def collect(k, value):
        exchange(k).wait_recv()
        return value + z_buf[k].astype(F32)

    total = lax.fori_loop(1, levels, collect, total)
    out_ref[...] = total.T.astype(BF16)
    for copy in copies:
        copy.wait_send()

    def drain(k, carry):
        exchange(k).wait_send()
        return carry

    lax.fori_loop(1, levels, drain, 0)


def reduce_grad(y, row_scale, cot, dp_count):
    slots, inner = y.shape
    width = cot.shape[1]
    share = width // dp_count
    levels = dp_count // RING
    some = levels // 2
    vmem = pl.BlockSpec(memory_space=pltpu.VMEM)
    dma = pltpu.SemaphoreType.DMA
    return pl.pallas_call(
        grad_kernel,
        name="grads",
        out_shape=jax.ShapeDtypeStruct((inner, share), BF16),
        in_specs=[vmem] * 3,
        out_specs=vmem,
        scratch_shapes=[
            pltpu.VMEM((slots, inner), BF16),
            pltpu.VMEM((levels, RING, share, inner), BF16),
            pltpu.VMEM((some, share, inner), BF16),
            pltpu.VMEM((some, share, inner), BF16),
            pltpu.VMEM((levels, share, inner), BF16),
            pltpu.VMEM((levels, share, inner), BF16),
            pltpu.VMEM((levels, share, inner), BF16),
            pltpu.VMEM((levels, share, inner), BF16),
            dma((6,)),
            dma((6,)),
            dma((levels,)),
            dma((levels,)),
        ],
        compiler_params=pltpu.CompilerParams(
            collective_id=2, has_side_effects=True, vmem_limit_bytes=60 * 1024 * 1024
        ),
    )(y, row_scale, cot)


def corner_turn(tokens, base_rows, baseline_owner):
    dp_count = lax.axis_size("dp")
    tok_rows, feat_width = tokens.shape
    slot_cap = 2 * tok_rows // dp_count
    own_slots = slot_cap * dp_count
    index, starts, ends, owner_start = layout_tables(base_rows, baseline_owner)
    local = jnp.arange(tok_rows, dtype=jnp.int32)
    inside = ((starts[None, :] <= local[:, None]) & (local[:, None] < ends[None, :])).astype(
        jnp.int32
    )
    row_start = jnp.sum(inside * starts[None, :], axis=1)
    row_owner = jnp.sum(inside * baseline_owner[None, :], axis=1)
    row_ostart = jnp.sum(inside * owner_start[None, :], axis=1)
    send_slot = row_owner * slot_cap + row_ostart + local - row_start
    outgoing = (
        jnp.zeros((own_slots, feat_width), jnp.bfloat16)
        .at[send_slot]
        .set(tokens)
        .reshape(dp_count, slot_cap, feat_width)
    )
    owner_index = lax.axis_index("dp")
    place = jnp.arange(slot_cap, dtype=jnp.int32)
    held = (
        (baseline_owner[None, :] == owner_index)
        & (owner_start[None, :] <= place[:, None])
        & (place[:, None] < owner_start[None, :] + base_rows[None, :])
    ).astype(jnp.int32)
    got_start = jnp.sum(held * owner_start[None, :], axis=1)
    got_len = jnp.sum(held * base_rows[None, :], axis=1)
    got_any = jnp.sum(held, axis=1)
    sender = jnp.arange(dp_count, dtype=jnp.int32)[:, None]
    recv_slot = (
        dp_count * got_start[None, :]
        + sender * got_len[None, :]
        + place[None, :]
        - got_start[None, :]
    )
    recv_slot = jnp.where(got_any[None, :] > 0, recv_slot, own_slots).reshape(-1)
    arrived = lax.all_to_all(outgoing, "dp", split_axis=0, concat_axis=0, tiled=True)
    return (
        jnp.zeros((own_slots, feat_width), jnp.bfloat16)
        .at[recv_slot]
        .set(arrived.reshape(-1, feat_width), mode="drop")
    )


def per_device(
    tokens,
    base_rows,
    baseline_owner,
    cotangent,
    *params,
):
    tables = (
        base_rows[:, None],
        base_rows[None, :],
        baseline_owner[:, None],
        baseline_owner[None, :],
    )
    stream = corner_turn(tokens, base_rows, baseline_owner)
    result, y, row_scale = run_blocks(tables, stream, tuple(item[0] for item in params))
    grad = reduce_grad(y, row_scale, cotangent[0], lax.axis_size("dp"))
    return (result[None], grad[None])


def solution(mesh):
    return jax.shard_map(
        per_device,
        mesh=mesh,
        in_specs=(
            P("dp", None),
            P(),
            P(),
            P("section", "dp", None),
            P("section", None),
            P("section", None, "tensor"),
            P("section", None, "tensor"),
            P("section", None, None),
            P("section", None, "tensor"),
            P("section", "tensor"),
            P("section", "tensor"),
            P("section", "tensor"),
            P("section", "tensor"),
            P("section", "tensor", None),
        ),
        out_specs=(P("section", "dp", None), P("section", "tensor", "dp")),
        check_vma=False,
    )
```

time: 648 us -> 194 us (0.30)
  waiting for transfers between devices: 407 us -> 44.5 us
  Pallas kernels: 0 us -> 116 us
  matrix products: 51.8 us -> 0 us
  local copies, waits for them, and re-layouts: 66.8 us -> 16.9 us
  other arithmetic: 45.6 us -> 2.88 us
  blocking collectives: 23.8 us -> 0 us
  loops' own time: 15.7 us -> 0 us
  between operations: 14.8 us -> 0.77 us
    reduce_scatter x4 -> x0, waiting for transfers between devices: 285 us -> none  [the longest x1 214 us: per_device(): lax.psum_scatter(grad_acc.astype(jnp.bfloat16), 'dp', scatter_dimension=1...]
    pallas_call x0 -> x2, Pallas kernels: none -> 116 us  [the longest x1 89.1 us: run_blocks(): pl.pallas_call(functools.partial(block_kernel, chunks, heads), name='bloc...]
    all_gather x3 -> x0, waiting for transfers between devices: 71.5 us -> none  [block_layer(): result = lax.all_gather(own_out, 'tensor', axis=0, tiled=True)]
    dot_general x66 -> x0, matrix products: 51.8 us -> none  [the longest x3 10 us: block_layer(): jnp.dot(y_norm, out_proj, preferred_element_type=jnp.float32)]
    psum x3 -> x0, blocking collectives: 23.8 us -> none  [block_layer(): sq_sum = lax.psum(jnp.sum(gated * gated, axis=-1), 'tensor')]
    convert_element_type x18 -> x0, other arithmetic: 17.9 us -> none  [the longest x3 9.48 us: block_layer(): rows_f = rows_in.astype(jnp.float32)]
    another operation x3 -> x0, loops' own time: 15.7 us -> none  [block_scan(): lax.scan(advance, (state, prev_segment), scanned)]
    dynamic_update_slice x24 -> x0, local copies, waits for them, and re-layouts: 10.5 us -> none  [block_scan(): lax.scan(advance, (state, prev_segment), scanned)]
  transfers between devices with their start and end apart: 10 -> 1, of which waited for: 10 -> 1; matrix products, arithmetic and copies ran while one was open for 3% -> 2% of each run, Pallas kernels for 0% -> 0%
where the time goes in v1:
time: 194 us; the launch traced here: 193 us
  Pallas kernels  116 us (60%)
  waiting for transfers between devices  44.5 us (23%)
  local copies, waits for them, and re-layouts  16.9 us (9%)
  starting transfers between devices  12.2 us (6%)
  other arithmetic  2.88 us (1%)
    pallas_call x1, Pallas kernels, run_blocks(): pl.pallas_call(functools.partial(block_kernel, chunks, heads), name='bloc...  89.1 us
    all_to_all x1, waiting for transfers between devices, corner_turn(): lax.all_to_all(outgoing, 'dp', split_axis=0, concat_axis=0, tiled=True)  44.5 us
    pallas_call x1, Pallas kernels, reduce_grad(): pl.pallas_call(grad_kernel, name='grads', out_shape=jax.ShapeDtypeStruct(...  26.9 us
    all_to_all x1, starting transfers between devices, corner_turn(): lax.all_to_all(outgoing, 'dp', split_axis=0, concat_axis=0, tiled=True)  12.2 us
    scatter x1, local copies, waits for them, and re-layouts, corner_turn(): return jnp.zeros((own_slots, feat_width), jnp.bfloat16).at[recv_slot].set...  5.1 us
    scatter x1, local copies, waits for them, and re-layouts, corner_turn(): outgoing = jnp.zeros((own_slots, feat_width), jnp.bfloat16).at[send_slot]...  4.4 us
  transfers between devices with their start and end apart: 1, of which 1 were waited for; matrix products, arithmetic and copies ran while one was open for 2% of the time, Pallas kernels for 0%

profile of v1, /device:TPU:1, one launch (start us, length us, event | category | flops | bytes accessed | tf_op | source)
XLA Modules:
  0.0 193.3 jit_solution(14922594260189170452)
XLA Ops:
  0.6 0.9 select_reduce_fusion.3
  1.5 0.8 copy.28.rows_c
  2.3 0.0 copy-start.1
  2.3 0.2 reduce-window.8
  2.5 0.1 reduce
  2.6 0.7 fusion.8
  3.3 0.8 select_reduce_fusion.2
  4.1 4.4 %scatter_custom_fusion = bf16[512,2048]{1,0:T(8,128)(2,1)} fusion(s32[256]{0:T(256)S(1)} %bitcast.36, bf16[256,2048]{1,0:T(8,128)(2,1)} %param.14, bf16[]{:T(256)} %constant.11.clone.1), kind=kCustom, calls=%fused_computation.4 | custom fusion | bytes 2097664 | tf_op jit(solution)/shard_map/scatter | solution.py:668
  8.5 0.0 copy-start.5
  8.5 0.0 copy-start.6
  8.5 0.0 copy-start.7
  8.5 0.0 copy-start.4
  8.5 0.0 copy-start.3
  8.6 0.0 copy-start.2
  8.6 0.0 copy-done.1
  8.6 12.2 %all-to-all-start = ((bf16[32,16,2048]{2,1,0:T(8,128)(2,1)}), bf16[32,16,2048]{2,1,0:T(8,128)(2,1)S(1)}, u32[]{:S(2)}, u32[]{:S(2)}) async-start(bf16[32,16,2048]{2,1,0:T(8,128)(2,1)} %bitcast.8), calls=%async_computation | async-start | bytes 4194304 | tf_op jit(solution)/shard_map/all_to_all | solution.py:689
  20.8 0.0 copy-done.5
  20.8 0.5 pad.15.step_bias
  21.3 0.0 copy-done.6
  21.3 0.6 pad.16.decay_log
  21.9 0.0 copy-done.7
  21.9 0.6 pad.17.skip_gain
  22.5 0.0 copy-done.4
  22.5 0.0 copy-done.3
  22.5 0.2 convert_reduce_fusion
  22.7 0.1 reshape.171
  22.8 0.7 copy.29.own_c
  23.5 0.0 copy-done.2
  23.5 0.3 copy.27
  23.8 0.9 pad.14.w_step
  24.7 44.5 %all-to-all-done = bf16[32,16,2048]{2,1,0:T(8,128)(2,1)S(1)} async-done(((bf16[32,16,2048]{2,1,0:T(8,128)(2,1)}), bf16[32,16,2048]{2,1,0:T(8,128)(2,1)S(1)}, u32[]{:S(2)}, u32[]{:S(2)}) %all-to-all-start) | async-done | bytes 2097184 | tf_op jit(solution)/shard_map/all_to_all | solution.py:689
  69.2 5.1 %scatter_custom_fusion.1.stream = bf16[512,2048]{1,0:T(8,128)(2,1)} fusion(s32[512]{0:T(512)S(1)} %bitcast.35, bf16[512,2048]{1,0:T(8,128)(2,1)S(1)} %bitcast.21, bf16[]{:T(256)} %constant.11.clone.1), kind=kCustom, calls=%fused_computation.2 | custom fusion | bytes 2097154 | tf_op jit(solution)/shard_map/scatter | solution.py:693
  74.3 89.1 %blocks.1 = (bf16[512,2048]{1,0:T(8,128)(2,1)}, bf16[512,512]{1,0:T(8,128)(2,1)}, f32[512,128]{1,0:T(8,128)}) custom-call(s32[128,1]{1,0:T(8,128)} %copy-done.1, s32[1,128]{1,0:T(1,128)} %bitcast.30, s32[128,1]{1,0:T(8,128)} %copy.29.own_c, s32[1,128]{1,0:T(1,128)} %bitcast.31, bf16[512,2048]{1,0:T(8,128)(2,1)} %scatter_custom_fusion.1.stream, ...), custom_call_target="tpu_custom_call" | custom-call | tf_op jit(solution)/shard_map/blocks/pallas_call | solution.py:434
  163.5 0.0 copy-start
  163.5 26.9 %grads.1 = bf16[512,64]{1,0:T(8,128)(2,1)} custom-call(bf16[512,512]{1,0:T(8,128)(2,1)} %get-tuple-element.6.y_ref, f32[512,128]{1,0:T(8,128)} %get-tuple-element.7.rs_ref, bf16[512,2048]{1,0:T(8,128)(2,1)} %bitcast.20), custom_call_target="tpu_custom_call" | custom-call | tf_op jit(solution)/shard_map/grads/pallas_call | solution.py:625
  190.4 1.6 copy.30
  192.0 0.0 copy-done
  192.0 1.3 copy.32
  (7 shorter events, 0.0 us)
Async XLA Ops:
  2.3 6.3 %copy-start.1 = (s32[128,1]{1,0:T(8,128)}, s32[128,1]{1,0:T(8,128)S(1)}, u32[]{:S(2)}) copy-start(s32[128,1]{1,0:T(8,128)S(1)} %copy.28.rows_c) | copy-start | bytes 1540
  8.5 12.2 %copy-start.5 = (f32[1,8]{1,0:T(1,128)S(1)}, f32[1,8]{1,0:T(1,128)}, u32[]{:S(2)}) copy-start(f32[1,8]{1,0:T(1,128)} %param.23) | copy-start | bytes 100
  8.5 12.8 %copy-start.6 = (f32[1,8]{1,0:T(1,128)S(1)}, f32[1,8]{1,0:T(1,128)}, u32[]{:S(2)}) copy-start(f32[1,8]{1,0:T(1,128)} %param.24) | copy-start | bytes 100
  8.5 13.4 %copy-start.7 = (f32[1,8]{1,0:T(1,128)S(1)}, f32[1,8]{1,0:T(1,128)}, u32[]{:S(2)}) copy-start(f32[1,8]{1,0:T(1,128)} %param.25) | copy-start | bytes 100
  8.5 13.9 %copy-start.4 = (s32[128]{0:T(128)S(1)}, s32[128]{0:T(128)}, u32[]{:S(2)}) copy-start(s32[128]{0:T(128)} %param.16) | copy-start | bytes 1540
  8.5 13.9 %copy-start.3 = (s32[128]{0:T(128)S(1)}, s32[128]{0:T(128)}, u32[]{:S(2)}) copy-start(s32[128]{0:T(128)} %param.15) | copy-start | bytes 1540
  8.6 14.9 %copy-start.2 = (bf16[1,2048,8]{1,2,0:T(8,128)(2,1)S(1)}, bf16[1,2048,8]{1,2,0:T(8,128)(2,1)}, u32[]{:S(2)}) copy-start(bf16[1,2048,8]{1,2,0:T(8,128)(2,1)} %param.22) | copy-start | bytes 98308
  8.6 60.7 %all-to-all-start = ((bf16[32,16,2048]{2,1,0:T(8,128)(2,1)}), bf16[32,16,2048]{2,1,0:T(8,128)(2,1)S(1)}, u32[]{:S(2)}, u32[]{:S(2)}) async-start(bf16[32,16,2048]{2,1,0:T(8,128)(2,1)} %bitcast.8), calls=%async_computation | async-start | bytes 4194304 | tf_op jit(solution)/shard_map/all_to_all | solution.py:689
  163.5 28.6 %copy-start = (bf16[512,2048]{1,0:T(8,128)(2,1)S(1)}, bf16[512,2048]{1,0:T(8,128)(2,1)}, u32[]{:S(2)}) copy-start(bf16[512,2048]{1,0:T(8,128)(2,1)} %get-tuple-element.5) | copy-start | bytes 6291460

commit v2 on v1

--- a/solution.py
+++ b/solution.py
@@ -17,18 +17,6 @@
 BF16 = jnp.bfloat16
 
 
-def layout_tables(base_rows, baseline_owner):
-    count = base_rows.shape[0]
-    index = jnp.arange(count, dtype=jnp.int32)
-    ends = jnp.cumsum(base_rows)
-    starts = ends - base_rows
-    earlier = (baseline_owner[:, None] == baseline_owner[None, :]) & (
-        index[None, :] < index[:, None]
-    )
-    owner_start = jnp.sum(jnp.where(earlier, base_rows[None, :], 0), axis=1)
-    return (index, starts, ends, owner_start)
-
-
 def iota(shape, axis):
     return lax.broadcasted_iota(jnp.int32, shape, axis)
 
@@ -57,20 +45,29 @@
     rows_r,
     own_c,
     own_r,
-    stream,
     pre_gain,
+    step_bias,
+    decay_log,
+    skip_gain,
+    norm_gain,
+    tokens,
+    in_hbm,
+    gate_hbm,
+    state_hbm,
+    step_hbm,
+    out_hbm,
+    out_ref,
+    y_ref,
+    rs_ref,
     w_in,
     w_gate,
     w_state,
     w_step,
-    step_bias,
-    decay_log,
-    skip_gain,
-    norm_gain,
     w_out,
-    out_ref,
-    y_ref,
-    rs_ref,
+    tok_buf,
+    away,
+    arrived,
+    s_buf,
     u_buf,
     o_buf,
     p_buf,
@@ -89,6 +86,10 @@
     seg_row,
     sq_buf,
     skip_row,
+    load_sem,
+    turn_send,
+    turn_recv,
+    feed_send,
     hand_sem,
     hand_send,
     out_sem,
@@ -103,18 +104,52 @@
     sec = lax.axis_index("section")
     owner = lax.axis_index("dp")
     right, left, opposite = ((me + 1) % RING, (me + 3) % RING, (me + 2) % RING)
-    width = o_buf.shape[1]
     readers = lax.axis_size("dp")
     inner = w_in.shape[1]
     pairs = heads // 2
     piece = ROWS // RING
     half = piece // 2
     count = rows_r.shape[1]
+    slots = chunks * ROWS
+    cap = slots // readers
+    tok_rows, part = tok_buf.shape
+    my_cols = pl.ds(pl.multiple_of((2 * me + sec) * part, part), part)
+
+    loads = [
+        pltpu.make_async_copy(src, dst, load_sem.at[k])
+        for k, (src, dst) in enumerate(
+            (
+                (tokens.at[:, my_cols], tok_buf),
+                (in_hbm, w_in),
+                (state_hbm, w_state),
+                (step_hbm, w_step),
+                (gate_hbm, w_gate),
+                (out_hbm, w_out),
+            )
+        )
+    ]
+    for load in loads:
+        load.start()
 
     barrier = pltpu.get_barrier_semaphore()
-    for other in (right, left, opposite):
-        pl.semaphore_signal(barrier, inc=1, device_id={"tensor": other}, device_id_type=MESH)
-    pl.semaphore_signal(barrier, inc=1, device_id={"section": 1 - sec}, device_id_type=MESH)
+
+    def greet(k, carry):
+        pl.semaphore_signal(
+            barrier, inc=1, device_id={"dp": (owner + k) % readers}, device_id_type=MESH
+        )
+        return carry
+
+    lax.fori_loop(1, readers, greet, 0)
+    for k in range(RING):
+        other = (me + k) % RING
+        if k:
+            pl.semaphore_signal(barrier, inc=1, device_id={"tensor": other}, device_id_type=MESH)
+        pl.semaphore_signal(
+            barrier,
+            inc=1,
+            device_id={"section": 1 - sec, "tensor": other},
+            device_id_type=MESH,
+        )
 
     def rows_of(t):
         return pl.ds(pl.multiple_of(t * ROWS, ROWS), ROWS)
@@ -129,39 +164,83 @@
             return pl.ds(pl.multiple_of(t * ROWS + who * piece, piece), piece)
         return pl.ds(pl.multiple_of(t * ROWS + who * piece + which * half, half), half)
 
-    def push(src, dst, send_sem, recv_sem, who):
+    def cap_of(who):
+        return pl.ds(pl.multiple_of(who * cap, cap), cap)
+
+    def push(src, dst, send_sem, recv_sem, **where):
         return pltpu.make_async_remote_copy(
             src_ref=src,
             dst_ref=dst,
             send_sem=send_sem,
             recv_sem=recv_sem,
-            device_id={"tensor": who},
+            device_id=where,
             device_id_type=MESH,
         )
 
-    def feed(t):
-        return pltpu.make_async_copy(stream.at[rows_of(t)], u_buf.at[rows_of(t)], hand_sem.at[t])
-
-    def hand_over(t):
-        return pltpu.make_async_remote_copy(
-            src_ref=o_buf.at[rows_of(t)],
-            dst_ref=u_buf.at[rows_of(t)],
-            send_sem=hand_send.at[t],
-            recv_sem=hand_sem.at[t],
-            device_id={"section": 1 - sec},
-            device_id_type=MESH,
-        )
+    def turn(k):
+        other = (owner + k) % readers
+        return push(
+            away.at[cap_of(other)],
+            arrived.at[cap_of(owner)],
+            turn_send.at[k],
+            turn_recv.at[k],
+            dp=other,
+        )
+
+    def feed_own(t):
+        return pltpu.make_async_copy(s_buf.at[t], u_buf.at[rows_of(t), my_cols], hand_sem.at[t])
+
+    def feed(t, k):
+        return push(
+            s_buf.at[t],
+            u_buf.at[rows_of(t), my_cols],
+            feed_send.at[k, t],
+            hand_sem.at[t],
+            section=0,
+            tensor=(me + k) % RING,
+        )
+
+    def hand_over(t, k):
+        where = (
+            lambda: out_piece(t, me),
+            lambda: out_piece(t, left),
+            lambda: out_piece(t, right),
+            lambda: out_piece(t, opposite, 0),
+            lambda: out_piece(t, opposite, 1),
+        )[k]()
+        return push(
+            o_buf.at[where], u_buf.at[where], hand_send.at[k, t], hand_sem.at[t], section=1 - sec
+        )
+
+    def pass_on(t, *which):
+        @pl.when(sec == 0)
+        def _():
+            for k in which:
+                hand_over(t, k).start()
 
     def store_out(t):
         return pltpu.make_async_copy(o_buf.at[rows_of(t)], out_ref.at[rows_of(t)], out_sem.at[t])
 
-    @pl.when(sec == 0)
-    def _():
-        for t in range(chunks):
-            feed(t).start()
-
     start_row, start_col = owner_starts(rows_c[...], rows_r[...], own_c[...], own_r[...])
-    slots = chunks * ROWS
+    down, across = iota((count, count), 0), iota((count, count), 1)
+    first_c = jnp.sum(jnp.where(across < down, rows_r[...], 0), axis=1, keepdims=True)
+    token = iota((count, tok_rows), 1)
+    inside = (token >= first_c) & (token < first_c + rows_c[...])
+    target = jnp.sum(
+        jnp.where(inside, own_c[...] * cap + start_col - first_c + token, 0), axis=0, keepdims=True
+    )
+    chosen = (iota((slots, tok_rows), 0) == target).astype(F32).astype(BF16)
+    loads[0].wait()
+    away[...] = jnp.dot(chosen, tok_buf[...], preferred_element_type=F32).astype(BF16)
+    arrived[cap_of(owner), :] = away[cap_of(owner), :]
+    pl.semaphore_wait(barrier, readers - 1 + RING - 1 + RING)
+
+    def send_turn(k, carry):
+        turn(k).start()
+        return carry
+
+    lax.fori_loop(1, readers, send_turn, 0)
+
     ids_c = (iota((count, 1), 0) + 1).astype(F32)
     ids_r = (iota((1, count), 1) + 1).astype(F32)
     slot_r = iota((count, slots), 1)
@@ -181,6 +260,13 @@
     )
     ids_col = jnp.sum(jnp.where(held_r, ids_r, 0.0), axis=1, keepdims=True)
     seg_col[...] = jnp.broadcast_to(ids_col, (slots, ROWS))
+    place, reader = slot_r % cap, slot_r // cap
+    held = (own_c[...] == owner) & (place >= start_col) & (place < start_col + rows_c[...])
+    goal = jnp.sum(
+        jnp.where(held, (readers - 1) * start_col + reader * rows_c[...] + place + 1, 0),
+        axis=0,
+        keepdims=True,
+    ) - 1
     state[...] = jnp.zeros_like(state)
     prev[...] = jnp.full(prev.shape, -1.0, F32)
     lane = iota((ROWS, 128), 1)
@@ -197,7 +283,28 @@
             jnp.broadcast_to(skip_gain[...], (8, 128)), pair
         )
     rate = -jnp.exp(decay_log[...])
-    pl.semaphore_wait(barrier, 4)
+
+    def take_turn(k, carry):
+        turn(k).wait_recv()
+        return carry
+
+    lax.fori_loop(1, readers, take_turn, 0)
+    for t in range(chunks):
+        placed = (iota((ROWS, slots), 0) + t * ROWS == goal).astype(F32).astype(BF16)
+        s_buf[t] = jnp.dot(placed, arrived[...], preferred_element_type=F32).astype(BF16)
+        for k in range(1, RING):
+            feed(t, k).start()
+
+        @pl.when(sec == 0)
+        def _():
+            feed_own(t).start()
+
+        @pl.when(sec == 1)
+        def _():
+            feed(t, 0).start()
+
+    for load in loads[1:]:
+        load.wait()
 
     def stage_in(t):
         pltpu.make_async_copy(u_buf.at[rows_of(t)], u_buf.at[rows_of(t)], hand_sem.at[t]).wait()
@@ -265,69 +372,60 @@
         prev[...] = jnp.broadcast_to(last, prev.shape)
         sq_buf[0, t] = jnp.broadcast_to(jnp.sum(squares.T, axis=0, keepdims=True), (8, ROWS))
 
-    def send_squares(t):
-        return [
-            push(
-                sq_buf.at[0, t],
-                sq_buf.at[k, t],
-                sq_send.at[k - 1, t],
-                sq_recv.at[k - 1, t],
-                (me + k) % RING,
-            )
-            for k in range(1, RING)
-        ]
-
-    def reduce_copies(t):
-        mine = p_buf.at[t]
-        return (
-            push(mine.at[piece_of(opposite, 0)], a1.at[t], rs_send.at[0, t], rs_recv.at[0, t], right),
-            push(mine.at[piece_of(opposite, 1)], b1.at[t], rs_send.at[1, t], rs_recv.at[1, t], left),
-            push(mine.at[piece_of(right, 1)], a2.at[t, 1], rs_send.at[2, t], rs_recv.at[2, t], right),
-            push(mine.at[piece_of(left, 0)], b2.at[t, 0], rs_send.at[3, t], rs_recv.at[3, t], left),
-            push(mine.at[piece_of(right, 0)], a2.at[t, 0], rs_send.at[4, t], rs_recv.at[4, t], right),
-            push(mine.at[piece_of(left, 1)], b2.at[t, 1], rs_send.at[5, t], rs_recv.at[5, t], left),
-        )
-
-    def gather_copies(t):
-        own, from_left, from_right = (
-            o_buf.at[out_piece(t, me)],
-            o_buf.at[out_piece(t, left, 0)],
-            o_buf.at[out_piece(t, right, 1)],
-        )
-        return (
-            push(own, own, ag_send.at[0, t], ag_recv.at[0, t], right),
-            push(own, own, ag_send.at[1, t], ag_recv.at[1, t], left),
-            push(from_left, from_left, ag_send.at[2, t], ag_recv.at[2, t], right),
-            push(from_right, from_right, ag_send.at[3, t], ag_recv.at[3, t], left),
-        )
+    def square_copy(t, k):
+        return push(
+            sq_buf.at[0, t],
+            sq_buf.at[k, t],
+            sq_send.at[k - 1, t],
+            sq_recv.at[k - 1, t],
+            tensor=(me + k) % RING,
+        )
+
+    def reduce_copy(t, k):
+        who, which, dst, to = (
+            (opposite, 0, lambda: a1.at[t], right),
+            (opposite, 1, lambda: b1.at[t], left),
+            (right, 1, lambda: a2.at[t, 1], right),
+            (left, 0, lambda: b2.at[t, 0], left),
+            (right, 0, lambda: a2.at[t, 0], right),
+            (left, 1, lambda: b2.at[t, 1], left),
+        )[k]
+        return push(
+            p_buf.at[t, piece_of(who, which)], dst(), rs_send.at[k, t], rs_recv.at[k, t], tensor=to
+        )
+
+    def gather_copy(t, k):
+        where, to = (
+            (lambda: out_piece(t, me), right),
+            (lambda: out_piece(t, me), left),
+            (lambda: out_piece(t, left, 0), right),
+            (lambda: out_piece(t, right, 1), left),
+        )[k]
+        rows = o_buf.at[where()]
+        return push(rows, rows, ag_send.at[k, t], ag_recv.at[k, t], tensor=to)
 
     def stage_out(t):
         p_buf[t] = jnp.dot(y_ref[rows_of(t), :], w_out[...], preferred_element_type=F32).astype(
             BF16
         )
-        for copy in reduce_copies(t)[:4]:
-            copy.start()
+        for k in range(4):
+            reduce_copy(t, k).start()
 
     def reduce_second(t):
-        copies = reduce_copies(t)
-        copies[0].wait_recv()
-        where = piece_of(right, 0)
-        p_buf[t, where, :] = (p_buf[t, where, :].astype(F32) + a1[t].astype(F32)).astype(BF16)
-        copies[4].start()
-        copies[1].wait_recv()
-        where = piece_of(left, 1)
-        p_buf[t, where, :] = (p_buf[t, where, :].astype(F32) + b1[t].astype(F32)).astype(BF16)
-        copies[5].start()
+        for k, who, which, got in ((0, right, 0, a1), (1, left, 1, b1)):
+            reduce_copy(t, k).wait_recv()
+            where = piece_of(who, which)
+            p_buf[t, where, :] = (p_buf[t, where, :].astype(F32) + got[t].astype(F32)).astype(BF16)
+            reduce_copy(t, k + 4).start()
 
     def reduce_last(t):
-        for copy in send_squares(t):
-            copy.wait_recv()
+        for k in range(1, RING):
+            square_copy(t, k).wait_recv()
         total = sq_buf[0, t] + sq_buf[1, t] + sq_buf[2, t] + sq_buf[3, t]
         scale = lax.rsqrt(total / (RING * inner) + EPS)
         rs_ref[rows_of(t), :] = jnp.broadcast_to(scale[0:1, :], (ROWS, ROWS)).T
-        copies = reduce_copies(t)
-        for copy in copies[2:]:
-            copy.wait_recv()
+        for k in range(2, 6):
+            reduce_copy(t, k).wait_recv()
         for which in (0, 1):
             where = out_piece(t, me, which)
             summed = (
@@ -338,69 +436,77 @@
             o_buf[where, :] = (
                 u_buf[where, :].astype(F32) + rs_ref[where, 0:1] * summed
             ).astype(BF16)
-        for copy in gather_copies(t)[:2]:
-            copy.start()
+        gather_copy(t, 0).start()
+        gather_copy(t, 1).start()
+        pass_on(t, 0)
 
     def gather_second(t):
-        copies = gather_copies(t)
-        copies[0].wait_recv()
-        copies[2].start()
-        copies[1].wait_recv()
-        copies[3].start()
+        for k in (0, 1):
+            gather_copy(t, k).wait_recv()
+            gather_copy(t, k + 2).start()
+        pass_on(t, 1, 2)
 
     def gather_last(t):
-        copies = gather_copies(t)
-        copies[2].wait_recv()
-        copies[3].wait_recv()
+        gather_copy(t, 2).wait_recv()
+        gather_copy(t, 3).wait_recv()
+        pass_on(t, 3, 4)
+        store_out(t).start()
+
+    def step(t, carry):
+        @pl.when(t >= 4)
+        def _():
+            gather_last(t - 4)
+
+        @pl.when((t >= 3) & (t < chunks + 3))
+        def _():
+            gather_second(t - 3)
+
+        @pl.when((t >= 2) & (t < chunks + 2))
+        def _():
+            reduce_last(t - 2)
+
+        @pl.when(t < chunks)
+        def _():
+            stage_in(t)
+
+        @pl.when((t >= 1) & (t < chunks + 1))
+        def _():
+            reduce_second(t - 1)
+
+        @pl.when(t < chunks)
+        def _():
+            stage_scan(t)
+            for k in range(1, RING):
+                square_copy(t, k).start()
+            stage_out(t)
+
+        return carry
+
+    lax.fori_loop(0, chunks + 4, step, 0)
+
+    def sent_turn(k, carry):
+        turn(k).wait_send()
+        return carry
+
+    lax.fori_loop(1, readers, sent_turn, 0)
+
+    def drain(t, carry):
+        for k in range(6):
+            reduce_copy(t, k).wait_send()
+        for k in range(4):
+            gather_copy(t, k).wait_send()
+        for k in range(1, RING):
+            square_copy(t, k).wait_send()
+            feed(t, k).wait_send()
 
         @pl.when(sec == 0)
         def _():
-            hand_over(t).start()
-
-        store_out(t).start()
-
-    def step(t, carry):
-        @pl.when(t < chunks)
-        def _():
-            stage_in(t)
-
-        @pl.when(t >= 2)
-        def _():
-            gather_last(t - 2)
-
-        @pl.when((t >= 1) & (t <= chunks))
-        def _():
-            reduce_second(t - 1)
-
-        @pl.when(t < chunks)
-        def _():
-            stage_scan(t)
-            for copy in send_squares(t):
-                copy.start()
-
-        @pl.when((t >= 1) & (t <= chunks))
-        def _():
-            reduce_last(t - 1)
-
-        @pl.when(t < chunks)
-        def _():
-            stage_out(t)
-
-        @pl.when((t >= 1) & (t <= chunks))
-        def _():
-            gather_second(t - 1)
-
-        return carry
-
-    lax.fori_loop(0, chunks + 2, step, 0)
-
-    def drain(t, carry):
-        for copy in reduce_copies(t) + gather_copies(t) + tuple(send_squares(t)):
-            copy.wait_send()
-
-        @pl.when(sec == 0)
-        def _():
-            hand_over(t).wait_send()
+            for k in range(5):
+                hand_over(t, k).wait_send()
+
+        @pl.when(sec == 1)
+        def _():
+            feed(t, 0).wait_send()
 
         store_out(t).wait()
         return carry
@@ -408,7 +514,7 @@
     lax.fori_loop(0, chunks, drain, 0)
 
 
-def run_blocks(tables, stream, params):
+def run_blocks(tables, tokens, params):
     (
         pre_gain,
         input_proj,
@@ -421,15 +527,17 @@
         norm_gain,
         out_proj,
     ) = params
-    slots, width = stream.shape
+    readers = lax.axis_size("dp")
+    tok_rows, width = tokens.shape
+    slots = 2 * tok_rows
     inner = input_proj.shape[1]
     heads = step_proj.shape[1]
     chunks = slots // ROWS
+    part = width // (2 * RING)
     pad = ((0, 0), (0, 128 - heads))
     vmem = pl.BlockSpec(memory_space=pltpu.VMEM)
     anywhere = pl.BlockSpec(memory_space=pl.ANY)
-    piece = ROWS // RING
-    half = piece // 2
+    half = ROWS // RING // 2
     dma = pltpu.SemaphoreType.DMA
     return pl.pallas_call(
         functools.partial(block_kernel, chunks, heads),
@@ -439,9 +547,18 @@
             jax.ShapeDtypeStruct((slots, inner), BF16),
             jax.ShapeDtypeStruct((slots, 128), F32),
         ),
-        in_specs=[vmem] * 4 + [anywhere] + [vmem] * 10,
+        in_specs=[vmem] * 9 + [anywhere] * 6,
         out_specs=(anywhere, vmem, vmem),
         scratch_shapes=[
+            pltpu.VMEM((width, inner), BF16),
+            pltpu.VMEM((width, inner), BF16),
+            pltpu.VMEM((width, 2 * NSTATE), BF16),
+            pltpu.VMEM((width, 128), BF16),
+            pltpu.VMEM((inner, width), BF16),
+            pltpu.VMEM((tok_rows, part), BF16),
+            pltpu.VMEM((slots, part), BF16),
+            pltpu.VMEM((slots, part), BF16),
+            pltpu.VMEM((chunks, ROWS, part), BF16),
             pltpu.VMEM((slots, width), BF16),
             pltpu.VMEM((slots, width), BF16),
             pltpu.VMEM((chunks, ROWS, width), BF16),
@@ -460,8 +577,12 @@
             pltpu.VMEM((chunks, 8, 128), F32),
             pltpu.VMEM((RING, chunks, 8, 128), F32),
             pltpu.VMEM((8, inner), F32),
+            dma((6,)),
+            dma((readers,)),
+            dma((readers,)),
+            dma((RING, chunks)),
             dma((chunks,)),
-            dma((chunks,)),
+            dma((5, chunks)),
             dma((chunks,)),
             dma((6, chunks)),
             dma((6, chunks)),
@@ -475,16 +596,16 @@
         ),
     )(
         *tables,
-        stream,
         pre_gain[None],
+        jnp.pad(step_bias[None], pad),
+        jnp.pad(decay_log[None], pad),
+        jnp.pad(skip_gain[None], pad),
+        norm_gain[None],
+        tokens,
         input_proj,
         gate_proj,
         state_proj,
         jnp.pad(step_proj, pad),
-        jnp.pad(step_bias[None], pad),
-        jnp.pad(decay_log[None], pad),
-        jnp.pad(skip_gain[None], pad),
-        norm_gain[None],
         out_proj,
     )
 
@@ -648,52 +769,6 @@
     )(y, row_scale, cot)
 
 
-def corner_turn(tokens, base_rows, baseline_owner):
-    dp_count = lax.axis_size("dp")
-    tok_rows, feat_width = tokens.shape
-    slot_cap = 2 * tok_rows // dp_count
-    own_slots = slot_cap * dp_count
-    index, starts, ends, owner_start = layout_tables(base_rows, baseline_owner)
-    local = jnp.arange(tok_rows, dtype=jnp.int32)
-    inside = ((starts[None, :] <= local[:, None]) & (local[:, None] < ends[None, :])).astype(
-        jnp.int32
-    )
-    row_start = jnp.sum(inside * starts[None, :], axis=1)
-    row_owner = jnp.sum(inside * baseline_owner[None, :], axis=1)
-    row_ostart = jnp.sum(inside * owner_start[None, :], axis=1)
-    send_slot = row_owner * slot_cap + row_ostart + local - row_start
-    outgoing = (
-        jnp.zeros((own_slots, feat_width), jnp.bfloat16)
-        .at[send_slot]
-        .set(tokens)
-        .reshape(dp_count, slot_cap, feat_width)
-    )
-    owner_index = lax.axis_index("dp")
-    place = jnp.arange(slot_cap, dtype=jnp.int32)
-    held = (
-        (baseline_owner[None, :] == owner_index)
-        & (owner_start[None, :] <= place[:, None])
-        & (place[:, None] < owner_start[None, :] + base_rows[None, :])
-    ).astype(jnp.int32)
-    got_start = jnp.sum(held * owner_start[None, :], axis=1)
-    got_len = jnp.sum(held * base_rows[None, :], axis=1)
-    got_any = jnp.sum(held, axis=1)
-    sender = jnp.arange(dp_count, dtype=jnp.int32)[:, None]
-    recv_slot = (
-        dp_count * got_start[None, :]
-        + sender * got_len[None, :]
-        + place[None, :]
-        - got_start[None, :]
-    )
-    recv_slot = jnp.where(got_any[None, :] > 0, recv_slot, own_slots).reshape(-1)
-    arrived = lax.all_to_all(outgoing, "dp", split_axis=0, concat_axis=0, tiled=True)
-    return (
-        jnp.zeros((own_slots, feat_width), jnp.bfloat16)
-        .at[recv_slot]
-        .set(arrived.reshape(-1, feat_width), mode="drop")
-    )
-
-
 def per_device(
     tokens,
     base_rows,
@@ -707,8 +782,7 @@
         baseline_owner[:, None],
         baseline_owner[None, :],
     )
-    stream = corner_turn(tokens, base_rows, baseline_owner)
-    result, y, row_scale = run_blocks(tables, stream, tuple(item[0] for item in params))
+    result, y, row_scale = run_blocks(tables, tokens, tuple(item[0] for item in params))
     grad = reduce_grad(y, row_scale, cotangent[0], lax.axis_size("dp"))
     return (result[None], grad[None])
 

time: 194 us -> 125 us (0.64)
  waiting for transfers between devices: 44.5 us -> 0 us
  starting transfers between devices: 12.2 us -> 0 us
  local copies, waits for them, and re-layouts: 16.9 us -> 11.2 us
  Pallas kernels: 116 us -> 113 us
  other arithmetic: 2.88 us -> 0 us
    all_to_all x1 -> x0, waiting for transfers between devices: 44.5 us -> none  [corner_turn(): lax.all_to_all(outgoing, 'dp', split_axis=0, concat_axis=0, tiled=True)]
    all_to_all x1 -> x0, starting transfers between devices: 12.2 us -> none  [corner_turn(): lax.all_to_all(outgoing, 'dp', split_axis=0, concat_axis=0, tiled=True)]
    scatter x2 -> x0, local copies, waits for them, and re-layouts: 9.5 us -> none  [the longest x1 5.1 us: corner_turn(): return jnp.zeros((own_slots, feat_width), jnp.bfloat16).at[recv_slot].set...]
    pallas_call x1, Pallas kernels: 89.1 us -> 85.2 us  [run_blocks(): pl.pallas_call(functools.partial(block_kernel, chunks, heads), name='bloc...]
    unnamed x19 -> x5, local copies, waits for them, and re-layouts: 3.25 us -> 3.97 us
  transfers between devices with their start and end apart: 1 -> 0, of which waited for: 1 -> 0; matrix products, arithmetic and copies ran while one was open for 2% -> 0% of each run, Pallas kernels for 0% -> 0%
where the time goes in v2:
time: 125 us
  Pallas kernels  113 us (90%)
  local copies, waits for them, and re-layouts  11.2 us (9%)
    pallas_call x1, Pallas kernels, run_blocks(): pl.pallas_call(functools.partial(block_kernel, chunks, heads), name='bloc...  85.2 us
    pallas_call x1, Pallas kernels, reduce_grad(): pl.pallas_call(grad_kernel, name='grads', out_shape=jax.ShapeDtypeStruct(...  27.8 us
    unnamed x5, local copies, waits for them, and re-layouts  3.97 us

profile of v2, /device:TPU:1, one launch (start us, length us, event | category | flops | bytes accessed | tf_op | source)
XLA Modules:
  0.0 124.8 jit_solution(283857821455339719)
XLA Ops:
  0.6 1.0 copy.16
  1.7 0.9 pad.17.step_hbm
  2.6 1.4 %copy.17.rows_c = s32[128,1]{1,0:T(8,128)} copy(s32[128,1]{0,1:T(1,128)} %bitcast.20) | data formatting | bytes 1024 | tf_op jit(solution)/shard_map/broadcast_in_dim | solution.py:780
  4.0 1.4 %copy.18.own_c = s32[128,1]{1,0:T(8,128)} copy(s32[128,1]{0,1:T(1,128)} %bitcast.22) | data formatting | bytes 1024 | tf_op jit(solution)/shard_map/broadcast_in_dim | solution.py:782
  5.3 1.1 pad.14.step_bias
  6.5 1.2 pad.15.decay_log
  7.7 1.2 pad.16.skip_gain
  8.9 85.2 %blocks.1 = (bf16[512,2048]{1,0:T(8,128)(2,1)}, bf16[512,512]{1,0:T(8,128)(2,1)}, f32[512,128]{1,0:T(8,128)}) custom-call(s32[128,1]{1,0:T(8,128)} %copy.17.rows_c, s32[1,128]{1,0:T(1,128)} %bitcast.21, s32[128,1]{1,0:T(8,128)} %copy.18.own_c, s32[1,128]{1,0:T(1,128)} %bitcast.23, f32[1,2048]{1,0:T(1,128)} %pre_gain.1, f32[1,128]{1,0:T(1,128)} %pad.14.step_bias, ...), custom_call_target="tpu_custom_call" | custom-call | tf_op jit(solution)/shard_map/blocks/pallas_call | solution.py:542
  94.0 0.0 copy-start
  94.0 27.8 %grads.1 = bf16[512,64]{1,0:T(8,128)(2,1)} custom-call(bf16[512,512]{1,0:T(8,128)(2,1)} %get-tuple-element.6.y_ref, f32[512,128]{1,0:T(8,128)} %get-tuple-element.7.rs_ref, bf16[512,2048]{1,0:T(8,128)(2,1)} %bitcast.15), custom_call_target="tpu_custom_call" | custom-call | tf_op jit(solution)/shard_map/grads/pallas_call | solution.py:746
  121.8 1.6 %copy.19 = bf16[1,512,64]{1,2,0:T(8,128)(2,1)} copy(bf16[1,512,64]{2,1,0:T(8,128)(2,1)} %bitcast.19) | data formatting | bytes 131072
  123.5 0.0 copy-done
  123.5 1.3 %copy.21 = bf16[1,512,2048]{2,1,0:T(8,128)(2,1)} copy(bf16[1,512,2048]{2,1,0:T(8,128)(2,1)S(1)} %bitcast.16) | data formatting | bytes 4194304
Async XLA Ops:
  94.0 29.4 %copy-start = (bf16[512,2048]{1,0:T(8,128)(2,1)S(1)}, bf16[512,2048]{1,0:T(8,128)(2,1)}, u32[]{:S(2)}) copy-start(bf16[512,2048]{1,0:T(8,128)(2,1)} %get-tuple-element.5) | copy-start | bytes 6291460

commit v3 on v2

--- a/solution.py
+++ b/solution.py
@@ -41,33 +41,34 @@
 def block_kernel(
     chunks,
     heads,
-    rows_c,
+    levels,
     rows_r,
-    own_c,
     own_r,
     pre_gain,
     step_bias,
     decay_log,
     skip_gain,
     norm_gain,
+    step_t,
     tokens,
     in_hbm,
     gate_hbm,
     state_hbm,
-    step_hbm,
     out_hbm,
+    cot_hbm,
     out_ref,
-    y_ref,
-    rs_ref,
+    grad_ref,
     w_in,
     w_gate,
     w_state,
     w_step,
     w_out,
+    small,
     tok_buf,
     away,
     arrived,
     s_buf,
+    r_buf,
     u_buf,
     o_buf,
     p_buf,
@@ -80,16 +81,33 @@
     gate_buf,
     bc_buf,
     dt_buf,
+    y_ref,
+    yn_buf,
+    rs_ref,
     state,
     prev,
     seg_col,
     seg_row,
     sq_buf,
     skip_row,
+    cot,
+    cot_t,
+    g_acc,
+    g_buf,
+    ga1,
+    gb1,
+    ga2,
+    gb2,
+    h_buf,
+    z_buf,
     load_sem,
     turn_send,
     turn_recv,
     feed_send,
+    side_recv,
+    relay_send,
+    relay_recv,
+    fill_send,
     hand_sem,
     hand_send,
     out_sem,
@@ -99,6 +117,10 @@
     ag_recv,
     sq_send,
     sq_recv,
+    g_send,
+    g_recv,
+    z_send,
+    z_recv,
 ):
     me = lax.axis_index("tensor")
     sec = lax.axis_index("section")
@@ -114,6 +136,12 @@
     cap = slots // readers
     tok_rows, part = tok_buf.shape
     my_cols = pl.ds(pl.multiple_of((2 * me + sec) * part, part), part)
+    my_z, my_y = owner // RING, owner % RING
+    right_y, left_y, opposite_y = ((my_y + 1) % RING, (my_y + 3) % RING, (my_y + 2) % RING)
+    share = g_buf.shape[2]
+    block = RING * share
+    group = levels // 2
+    some = group // 2
 
     loads = [
         pltpu.make_async_copy(src, dst, load_sem.at[k])
@@ -122,9 +150,9 @@
                 (tokens.at[:, my_cols], tok_buf),
                 (in_hbm, w_in),
                 (state_hbm, w_state),
-                (step_hbm, w_step),
                 (gate_hbm, w_gate),
                 (out_hbm, w_out),
+                (cot_hbm, cot),
             )
         )
     ]
@@ -190,15 +218,58 @@
     def feed_own(t):
         return pltpu.make_async_copy(s_buf.at[t], u_buf.at[rows_of(t), my_cols], hand_sem.at[t])
 
-    def feed(t, k):
+    def feed_core(t):
         return push(
             s_buf.at[t],
             u_buf.at[rows_of(t), my_cols],
-            feed_send.at[k, t],
+            feed_send.at[2, t],
             hand_sem.at[t],
             section=0,
-            tensor=(me + k) % RING,
-        )
+        )
+
+    def feed_side(t, k):
+        return push(
+            s_buf.at[t],
+            r_buf.at[t, :, my_cols],
+            feed_send.at[k, t],
+            side_recv.at[k, t],
+            section=1,
+            tensor=(right, left)[k],
+        )
+
+    def held_of(t, k, kind):
+        near, far = (left, right)[k], opposite
+        half_rows = pl.ds(k * (ROWS // 2), ROWS // 2)
+        who = far if kind == 2 else near
+        cols = pl.ds(pl.multiple_of(who * 2 * part, 2 * part), 2 * part)
+        if kind == 0:
+            return r_buf.at[t, :, cols], u_buf.at[rows_of(t), cols]
+        there = pl.ds(pl.multiple_of(t * ROWS + k * (ROWS // 2), ROWS // 2), ROWS // 2)
+        return r_buf.at[t, half_rows, cols], u_buf.at[there, cols]
+
+    def relay(t, k):
+        src, _ = held_of(t, k, 1)
+        return push(
+            src, src, relay_send.at[k, t], relay_recv.at[k, t], tensor=(right, left)[k]
+        )
+
+    def fill(t, k, kind):
+        src, dst = held_of(t, k, kind)
+        return push(src, dst, fill_send.at[k + kind, t], hand_sem.at[t], section=0)
+
+    def sides(t, carry):
+        for k in (0, 1):
+            here, _ = held_of(t, k, 0)
+            pltpu.make_async_copy(here, here, side_recv.at[k, t]).wait()
+            relay(t, k).start()
+            fill(t, k, 0).start()
+        return carry
+
+    def relayed(t, carry):
+        for k in (0, 1):
+            relay(t, k).wait_recv()
+            fill(t, k, 2).start()
+        return carry
 
     def hand_over(t, k):
         where = (
@@ -221,13 +292,17 @@
     def store_out(t):
         return pltpu.make_async_copy(o_buf.at[rows_of(t)], out_ref.at[rows_of(t)], out_sem.at[t])
 
-    start_row, start_col = owner_starts(rows_c[...], rows_r[...], own_c[...], own_r[...])
+    def column(row):
+        return jnp.broadcast_to(row.astype(F32), (count, count)).T[:, 0:1].astype(jnp.int32)
+
+    rows_c, own_c = column(rows_r[...]), column(own_r[...])
+    start_row, start_col = owner_starts(rows_c, rows_r[...], own_c, own_r[...])
     down, across = iota((count, count), 0), iota((count, count), 1)
     first_c = jnp.sum(jnp.where(across < down, rows_r[...], 0), axis=1, keepdims=True)
     token = iota((count, tok_rows), 1)
-    inside = (token >= first_c) & (token < first_c + rows_c[...])
+    inside = (token >= first_c) & (token < first_c + rows_c)
     target = jnp.sum(
-        jnp.where(inside, own_c[...] * cap + start_col - first_c + token, 0), axis=0, keepdims=True
+        jnp.where(inside, own_c * cap + start_col - first_c + token, 0), axis=0, keepdims=True
     )
     chosen = (iota((slots, tok_rows), 0) == target).astype(F32).astype(BF16)
     loads[0].wait()
@@ -245,9 +320,9 @@
     ids_r = (iota((1, count), 1) + 1).astype(F32)
     slot_r = iota((count, slots), 1)
     held_c = (
-        (own_c[...] == owner)
+        (own_c == owner)
         & (slot_r >= readers * start_col)
-        & (slot_r < readers * (start_col + rows_c[...]))
+        & (slot_r < readers * (start_col + rows_c))
     )
     ids_row = jnp.sum(jnp.where(held_c, ids_c, 0.0), axis=0, keepdims=True)
     for t in range(chunks):
@@ -261,9 +336,9 @@
     ids_col = jnp.sum(jnp.where(held_r, ids_r, 0.0), axis=1, keepdims=True)
     seg_col[...] = jnp.broadcast_to(ids_col, (slots, ROWS))
     place, reader = slot_r % cap, slot_r // cap
-    held = (own_c[...] == owner) & (place >= start_col) & (place < start_col + rows_c[...])
+    held = (own_c == owner) & (place >= start_col) & (place < start_col + rows_c)
     goal = jnp.sum(
-        jnp.where(held, (readers - 1) * start_col + reader * rows_c[...] + place + 1, 0),
+        jnp.where(held, (readers - 1) * start_col + reader * rows_c + place + 1, 0),
         axis=0,
         keepdims=True,
     ) - 1
@@ -278,11 +353,29 @@
         second = jnp.broadcast_to(value[:, 2 * pair + 1 : 2 * pair + 2], shape)
         return jnp.where(iota(shape, 1) < HEADDIM, first, second)
 
+    small[...] = jnp.zeros_like(small)
+    for k, ref in enumerate((step_bias, decay_log, skip_gain)):
+        small[k, 0:1, 0:heads] = ref[...]
+    w_step[...] = jnp.concatenate(
+        [step_t[...].astype(F32), jnp.zeros((128 - heads, step_t.shape[1]), F32)], axis=0
+    ).astype(BF16)
     for pair in range(pairs):
         skip_row[:, pair * 128 : (pair + 1) * 128] = spread(
-            jnp.broadcast_to(skip_gain[...], (8, 128)), pair
-        )
-    rate = -jnp.exp(decay_log[...])
+            jnp.broadcast_to(small[2, 0:1, :], (8, 128)), pair
+        )
+    rate = -jnp.exp(small[1, 0:1, :])
+
+    loads[5].wait()
+
+    def level_of(m):
+        return (my_z + m + 2) % levels
+
+    def turn_cot(m, carry):
+        cols = pl.ds(pl.multiple_of(level_of(m) * block, block), block)
+        cot_t[m] = cot[:, cols].T
+        return carry
+
+    lax.fori_loop(0, levels, turn_cot, 0)
 
     def take_turn(k, carry):
         turn(k).wait_recv()
@@ -292,8 +385,8 @@
     for t in range(chunks):
         placed = (iota((ROWS, slots), 0) + t * ROWS == goal).astype(F32).astype(BF16)
         s_buf[t] = jnp.dot(placed, arrived[...], preferred_element_type=F32).astype(BF16)
-        for k in range(1, RING):
-            feed(t, k).start()
+        feed_side(t, 0).start()
+        feed_side(t, 1).start()
 
         @pl.when(sec == 0)
         def _():
@@ -301,9 +394,24 @@
 
         @pl.when(sec == 1)
         def _():
-            feed(t, 0).start()
-
-    for load in loads[1:]:
+            feed_core(t).start()
+
+    @pl.when(sec == 1)
+    def _():
+        def relay_step(t, carry):
+            @pl.when(t < chunks)
+            def _():
+                sides(t, 0)
+
+            @pl.when(t >= 1)
+            def _():
+                relayed(t - 1, 0)
+
+            return carry
+
+        lax.fori_loop(0, chunks + 1, relay_step, 0)
+
+    for load in loads[1:5]:
         load.wait()
 
     def stage_in(t):
@@ -316,7 +424,10 @@
             BF16
         )
         dt_buf[...] = softplus(
-            jnp.dot(normed[...], w_step[...], preferred_element_type=F32) + step_bias[...]
+            lax.dot_general(
+                normed[...], w_step[...], (((1,), (1,)), ((), ())), preferred_element_type=F32
+            )
+            + small[0, 0:1, :]
         )
         gate_buf[...] = silu(jnp.dot(normed[...], w_gate[...], preferred_element_type=F32))
 
@@ -424,6 +535,9 @@
         total = sq_buf[0, t] + sq_buf[1, t] + sq_buf[2, t] + sq_buf[3, t]
         scale = lax.rsqrt(total / (RING * inner) + EPS)
         rs_ref[rows_of(t), :] = jnp.broadcast_to(scale[0:1, :], (ROWS, ROWS)).T
+        yn_buf[rows_of(t), :] = (
+            y_ref[rows_of(t), :].astype(F32) * rs_ref[rows_of(t), 0:1]
+        ).astype(BF16)
         for k in range(2, 6):
             reduce_copy(t, k).wait_recv()
         for which in (0, 1):
@@ -452,6 +566,65 @@
         pass_on(t, 3, 4)
         store_out(t).start()
 
+    early = (chunks - 1) * ROWS
+
+    def grad_early(m, carry):
+        g_acc[m] = jnp.dot(cot_t[m, :, :early], yn_buf[:early, :], preferred_element_type=F32)
+        return carry
+
+    def grad_late(m, carry):
+        term = g_acc[m] + jnp.dot(
+            cot_t[m, :, early:], yn_buf[early:, :], preferred_element_type=F32
+        )
+        g_buf[m] = term.astype(BF16).reshape(RING, share, inner)
+        return carry
+
+    def grad_copy(g, k):
+        base = g * group
+        first, second = pl.ds(base, some), pl.ds(base + some, some)
+        src, dst, to = (
+            (lambda: g_buf.at[first, opposite_y], lambda: ga1.at[g], right_y),
+            (lambda: g_buf.at[second, opposite_y], lambda: gb1.at[g], left_y),
+            (lambda: g_buf.at[second, right_y], lambda: ga2.at[second], right_y),
+            (lambda: g_buf.at[first, left_y], lambda: gb2.at[first], left_y),
+            (lambda: g_buf.at[first, right_y], lambda: ga2.at[first], right_y),
+            (lambda: g_buf.at[second, left_y], lambda: gb2.at[second], left_y),
+        )[k]
+        return push(src(), dst(), g_send.at[k, g], g_recv.at[k, g], dp=my_z * RING + to)
+
+    def exchange(m):
+        return push(
+            h_buf.at[m],
+            z_buf.at[m],
+            z_send.at[m],
+            z_recv.at[m],
+            dp=level_of(m) * RING + my_y,
+        )
+
+    def grad_send(g):
+        lax.fori_loop(g * group, (g + 1) * group, grad_late, 0)
+        for k in range(4):
+            grad_copy(g, k).start()
+
+    def grad_second(g):
+        for k, offset, who, got in ((0, 0, right_y, ga1), (1, some, left_y, gb1)):
+            grad_copy(g, k).wait_recv()
+            for j in range(some):
+                m = g * group + offset + j
+                g_buf[m, who] = (g_buf[m, who].astype(F32) + got[g, j].astype(F32)).astype(BF16)
+            grad_copy(g, k + 4).start()
+
+    def level_sum(m):
+        return g_buf[m, my_y].astype(F32) + ga2[m].astype(F32) + gb2[m].astype(F32)
+
+    def grad_finish(g):
+        for k in range(2, 6):
+            grad_copy(g, k).wait_recv()
+        for m in range(g * group, (g + 1) * group):
+            if m != levels - 2:
+                h_buf[m] = level_sum(m).astype(BF16)
+                exchange(m).start()
+
     def step(t, carry):
         @pl.when(t >= 4)
         def _():
@@ -480,9 +653,34 @@
                 square_copy(t, k).start()
             stage_out(t)
 
+        @pl.when(t == chunks)
+        def _():
+            lax.fori_loop(0, levels, grad_early, 0)
+
+        @pl.when(t == chunks + 1)
+        def _():
+            grad_send(0)
+            grad_send(1)
+
         return carry
 
     lax.fori_loop(0, chunks + 4, step, 0)
+    grad_second(0)
+    grad_second(1)
+    grad_finish(0)
+    grad_finish(1)
+    total = level_sum(levels - 2)
+    for m in range(levels):
+        if m != levels - 2:
+            exchange(m).wait_recv()
+            total = total + z_buf[m].astype(F32)
+    grad_ref[...] = total.astype(BF16)
+    for g in (0, 1):
+        for k in range(6):
+            grad_copy(g, k).wait_send()
+    for m in range(levels):
+        if m != levels - 2:
+            exchange(m).wait_send()
 
     def sent_turn(k, carry):
         turn(k).wait_send()
@@ -497,7 +695,8 @@
             gather_copy(t, k).wait_send()
         for k in range(1, RING):
             square_copy(t, k).wait_send()
-            feed(t, k).wait_send()
+        feed_side(t, 0).wait_send()
+        feed_side(t, 1).wait_send()
 
         @pl.when(sec == 0)
         def _():
@@ -506,7 +705,11 @@
 
         @pl.when(sec == 1)
         def _():
-            feed(t, 0).wait_send()
+            feed_core(t).wait_send()
+            for k in (0, 1):
+                relay(t, k).wait_send()
+                fill(t, k, 0).wait_send()
+                fill(t, k, 2).wait_send()
 
         store_out(t).wait()
         return carry
@@ -514,7 +717,7 @@
     lax.fori_loop(0, chunks, drain, 0)
 
 
-def run_blocks(tables, tokens, params):
+def run_blocks(tables, tokens, cot, params):
     (
         pre_gain,
         input_proj,
@@ -534,31 +737,34 @@
     heads = step_proj.shape[1]
     chunks = slots // ROWS
     part = width // (2 * RING)
-    pad = ((0, 0), (0, 128 - heads))
+    share = width // readers
+    levels = readers // RING
+    some = levels // 4
     vmem = pl.BlockSpec(memory_space=pltpu.VMEM)
     anywhere = pl.BlockSpec(memory_space=pl.ANY)
     half = ROWS // RING // 2
     dma = pltpu.SemaphoreType.DMA
     return pl.pallas_call(
-        functools.partial(block_kernel, chunks, heads),
+        functools.partial(block_kernel, chunks, heads, levels),
         name="blocks",
         out_shape=(
             jax.ShapeDtypeStruct((slots, width), BF16),
-            jax.ShapeDtypeStruct((slots, inner), BF16),
-            jax.ShapeDtypeStruct((slots, 128), F32),
+            jax.ShapeDtypeStruct((share, inner), BF16),
         ),
-        in_specs=[vmem] * 9 + [anywhere] * 6,
-        out_specs=(anywhere, vmem, vmem),
+        in_specs=[vmem] * 8 + [anywhere] * 6,
+        out_specs=(anywhere, vmem),
         scratch_shapes=[
             pltpu.VMEM((width, inner), BF16),
             pltpu.VMEM((width, inner), BF16),
             pltpu.VMEM((width, 2 * NSTATE), BF16),
-            pltpu.VMEM((width, 128), BF16),
+            pltpu.VMEM((128, width), BF16),
             pltpu.VMEM((inner, width), BF16),
+            pltpu.VMEM((3, 8, 128), F32),
             pltpu.VMEM((tok_rows, part), BF16),
             pltpu.VMEM((slots, part), BF16),
             pltpu.VMEM((slots, part), BF16),
             pltpu.VMEM((chunks, ROWS, part), BF16),
+            pltpu.VMEM((chunks, ROWS, width), BF16),
             pltpu.VMEM((slots, width), BF16),
             pltpu.VMEM((slots, width), BF16),
             pltpu.VMEM((chunks, ROWS, width), BF16),
@@ -571,16 +777,33 @@
             pltpu.VMEM((ROWS, inner), F32),
             pltpu.VMEM((ROWS, 2 * NSTATE), BF16),
             pltpu.VMEM((ROWS, 128), F32),
+            pltpu.VMEM((slots, inner), BF16),
+            pltpu.VMEM((slots, inner), BF16),
+            pltpu.VMEM((slots, 128), F32),
             pltpu.VMEM((NSTATE, inner), F32),
             pltpu.VMEM((8, 128), F32),
             pltpu.VMEM((slots, 128), F32),
             pltpu.VMEM((chunks, 8, 128), F32),
             pltpu.VMEM((RING, chunks, 8, 128), F32),
             pltpu.VMEM((8, inner), F32),
+            pltpu.VMEM((slots, width), BF16),
+            pltpu.VMEM((levels, RING * share, slots), BF16),
+            pltpu.VMEM((levels, RING * share, inner), F32),
+            pltpu.VMEM((levels, RING, share, inner), BF16),
+            pltpu.VMEM((2, some, share, inner), BF16),
+            pltpu.VMEM((2, some, share, inner), BF16),
+            pltpu.VMEM((levels, share, inner), BF16),
+            pltpu.VMEM((levels, share, inner), BF16),
+            pltpu.VMEM((levels, share, inner), BF16),
+            pltpu.VMEM((levels, share, inner), BF16),
             dma((6,)),
             dma((readers,)),
             dma((readers,)),
-            dma((RING, chunks)),
+            dma((3, chunks)),
+            dma((2, chunks)),
+            dma((2, chunks)),
+            dma((2, chunks)),
+            dma((4, chunks)),
             dma((chunks,)),
             dma((5, chunks)),
             dma((chunks,)),
@@ -590,6 +813,10 @@
             dma((4, chunks)),
             dma((3, chunks)),
             dma((3, chunks)),
+            dma((6, 2)),
+            dma((6, 2)),
+            dma((levels,)),
+            dma((levels,)),
         ],
         compiler_params=pltpu.CompilerParams(
             collective_id=1, has_side_effects=True, vmem_limit_bytes=60 * 1024 * 1024
@@ -597,176 +824,18 @@
     )(
         *tables,
         pre_gain[None],
-        jnp.pad(step_bias[None], pad),
-        jnp.pad(decay_log[None], pad),
-        jnp.pad(skip_gain[None], pad),
+        step_bias[None],
+        decay_log[None],
+        skip_gain[None],
         norm_gain[None],
+        step_proj.T,
         tokens,
         input_proj,
         gate_proj,
         state_proj,
-        jnp.pad(step_proj, pad),
         out_proj,
+        cot,
     )
-
-
-def grad_kernel(
-    y_ref,
-    rs_ref,
-    cot,
-    out_ref,
-    yn,
-    g_buf,
-    a1,
-    b1,
-    a2,
-    b2,
-    h_buf,
-    z_buf,
-    rs_send,
-    rs_recv,
-    z_send,
-    z_recv,
-):
-    levels, share = g_buf.shape[0], g_buf.shape[2]
-    index = lax.axis_index("dp")
-    my_z, my_y = index // RING, index % RING
-    right_y, left_y, opposite_y = ((my_y + 1) % RING, (my_y + 3) % RING, (my_y + 2) % RING)
-    right, left = my_z * RING + right_y, my_z * RING + left_y
-    block = RING * share
-    some = levels // 2
-
-    def level(k):
-        return ((my_z + k) % levels) * RING + my_y
-
-    barrier = pltpu.get_barrier_semaphore()
-    others = [right, left] + [level(k) for k in range(1, levels)]
-    for other in others:
-        pl.semaphore_signal(barrier, inc=1, device_id={"dp": other}, device_id_type=MESH)
-
-    yn[...] = (y_ref[...].astype(F32) * rs_ref[:, 0:1]).astype(BF16)
-
-    def push(src, dst, send_sem, recv_sem, who):
-        return pltpu.make_async_remote_copy(
-            src_ref=src,
-            dst_ref=dst,
-            send_sem=send_sem,
-            recv_sem=recv_sem,
-            device_id={"dp": who},
-            device_id_type=MESH,
-        )
-
-    low, high = pl.ds(0, some), pl.ds(some, some)
-    copies = (
-        push(g_buf.at[low, opposite_y], a1, rs_send.at[0], rs_recv.at[0], right),
-        push(g_buf.at[high, opposite_y], b1, rs_send.at[1], rs_recv.at[1], left),
-        push(g_buf.at[high, right_y], a2.at[high], rs_send.at[2], rs_recv.at[2], right),
-        push(g_buf.at[low, left_y], b2.at[low], rs_send.at[3], rs_recv.at[3], left),
-        push(g_buf.at[low, right_y], a2.at[low], rs_send.at[4], rs_recv.at[4], right),
-        push(g_buf.at[high, left_y], b2.at[high], rs_send.at[5], rs_recv.at[5], left),
-    )
-
-    def term(k, carry):
-        cols = pl.ds(pl.multiple_of(k * block, block), block)
-        product = lax.dot_general(
-            cot[:, cols], yn[...], (((0,), (0,)), ((), ())), preferred_element_type=F32
-        )
-        g_buf[k] = product.astype(BF16).reshape(RING, share, product.shape[1])
-        return carry
-
-    lax.fori_loop(0, some, term, 0)
-    pl.semaphore_wait(barrier, len(others))
-    copies[0].start()
-    copies[3].start()
-    lax.fori_loop(some, levels, term, 0)
-    copies[1].start()
-    copies[2].start()
-
-    copies[0].wait_recv()
-
-    def add_low(k, carry):
-        g_buf[k, right_y] = (g_buf[k, right_y].astype(F32) + a1[k].astype(F32)).astype(BF16)
-        return carry
-
-    lax.fori_loop(0, some, add_low, 0)
-    copies[4].start()
-    copies[1].wait_recv()
-
-    def add_high(k, carry):
-        g_buf[some + k, left_y] = (g_buf[some + k, left_y].astype(F32) + b1[k].astype(F32)).astype(
-            BF16
-        )
-        return carry
-
-    lax.fori_loop(0, some, add_high, 0)
-    copies[5].start()
-    for copy in copies[2:]:
-        copy.wait_recv()
-
-    def exchange(k):
-        return push(
-            h_buf.at[(my_z + k) % levels], z_buf.at[k], z_send.at[k], z_recv.at[k], level(k)
-        )
-
-    def finish(k, carry):
-        who = (my_z + k) % levels
-        h_buf[who] = (
-            g_buf[who, my_y].astype(F32) + a2[who].astype(F32) + b2[who].astype(F32)
-        ).astype(BF16)
-        exchange(k).start()
-        return carry
-
-    lax.fori_loop(1, levels, finish, 0)
-    total = g_buf[my_z, my_y].astype(F32) + a2[my_z].astype(F32) + b2[my_z].astype(F32)
-
-    def collect(k, value):
-        exchange(k).wait_recv()
-        return value + z_buf[k].astype(F32)
-
-    total = lax.fori_loop(1, levels, collect, total)
-    out_ref[...] = total.T.astype(BF16)
-    for copy in copies:
-        copy.wait_send()
-
-    def drain(k, carry):
-        exchange(k).wait_send()
-        return carry
-
-    lax.fori_loop(1, levels, drain, 0)
-
-
-def reduce_grad(y, row_scale, cot, dp_count):
-    slots, inner = y.shape
-    width = cot.shape[1]
-    share = width // dp_count
-    levels = dp_count // RING
-    some = levels // 2
-    vmem = pl.BlockSpec(memory_space=pltpu.VMEM)
-    dma = pltpu.SemaphoreType.DMA
-    return pl.pallas_call(
-        grad_kernel,
-        name="grads",
-        out_shape=jax.ShapeDtypeStruct((inner, share), BF16),
-        in_specs=[vmem] * 3,
-        out_specs=vmem,
-        scratch_shapes=[
-            pltpu.VMEM((slots, inner), BF16),
-            pltpu.VMEM((levels, RING, share, inner), BF16),
-            pltpu.VMEM((some, share, inner), BF16),
-            pltpu.VMEM((some, share, inner), BF16),
-            pltpu.VMEM((levels, share, inner), BF16),
-            pltpu.VMEM((levels, share, inner), BF16),
-            pltpu.VMEM((levels, share, inner), BF16),
-            pltpu.VMEM((levels, share, inner), BF16),
-            dma((6,)),
-            dma((6,)),
-            dma((levels,)),
-            dma((levels,)),
-        ],
-        compiler_params=pltpu.CompilerParams(
-            collective_id=2, has_side_effects=True, vmem_limit_bytes=60 * 1024 * 1024
-        ),
-    )(y, row_scale, cot)
 
 
 def per_device(
@@ -776,15 +845,11 @@
     cotangent,
     *params,
 ):
-    tables = (
-        base_rows[:, None],
-        base_rows[None, :],
-        baseline_owner[:, None],
-        baseline_owner[None, :],
+    tables = (base_rows[None, :], baseline_owner[None, :])
+    result, grad = run_blocks(
+        tables, tokens, cotangent[0], tuple(item[0] for item in params)
     )
-    result, y, row_scale = run_blocks(tables, tokens, tuple(item[0] for item in params))
-    grad = reduce_grad(y, row_scale, cotangent[0], lax.axis_size("dp"))
-    return (result[None], grad[None])
+    return (result[None], grad.T[None])
 
 
 def solution(mesh):

time: 125 us -> 106 us (0.85)
  Pallas kernels: 113 us -> 102 us
  local copies, waits for them, and re-layouts: 11.2 us -> 3.82 us
    pallas_call x2 -> x1, Pallas kernels: 113 us -> 102 us  [run_blocks(): pl.pallas_call(functools.partial(block_kernel, chunks, heads, levels), na...]
    pad x4 -> x0, local copies, waits for them, and re-layouts: 4.45 us -> none  [the longest x1 1.23 us: run_blocks(): jnp.pad(skip_gain[None], pad)]
    broadcast_in_dim x2 -> x0, local copies, waits for them, and re-layouts: 2.76 us -> none  [the longest x1 1.39 us: per_device(): base_rows[:, None]]
    unnamed x5 -> x4, local copies, waits for them, and re-layouts: 3.97 us -> 3.82 us
where the time goes in v3:
time: 106 us
  Pallas kernels  102 us (96%)
  local copies, waits for them, and re-layouts  3.82 us (4%)
    pallas_call x1, Pallas kernels, run_blocks(): pl.pallas_call(functools.partial(block_kernel, chunks, heads, levels), na...  102 us
    unnamed x4, local copies, waits for them, and re-layouts  3.82 us

profile of v3, /device:TPU:1, one launch (start us, length us, event | category | flops | bytes accessed | tf_op | source)
XLA Modules:
  0.0 106.2 jit_solution(4933465772677567345)
XLA Ops:
  0.6 101.7 %blocks.1 = (bf16[512,2048]{1,0:T(8,128)(2,1)}, bf16[64,512]{1,0:T(8,128)(2,1)}) custom-call(s32[1,128]{1,0:T(1,128)} %bitcast.22, s32[1,128]{1,0:T(1,128)} %bitcast.23, f32[1,2048]{1,0:T(1,128)} %pre_gain.1, f32[1,8]{1,0:T(1,128)} %step_bias.1, f32[1,8]{1,0:T(1,128)} %decay_log.1, f32[1,8]{1,0:T(1,128)} %skip_gain.1, f32[1,512]{1,0:T(1,128)} %norm_gain.1, ...), custom_call_target="tpu_custom_call" | custom-call | tf_op jit(solution)/shard_map/blocks/pallas_call | solution.py:747
  102.4 0.0 copy-start
  102.4 3.2 %copy.18 = bf16[1,512,2048]{2,1,0:T(8,128)(2,1)} copy(bf16[1,512,2048]{2,1,0:T(8,128)(2,1)} %bitcast.14) | data formatting | bytes 4194304
  105.6 0.0 copy-done
  105.6 0.6 copy.19
Async XLA Ops:
  102.4 3.2 %copy-start = (bf16[64,512]{1,0:T(8,128)(2,1)S(1)}, bf16[64,512]{1,0:T(8,128)(2,1)}, u32[]{:S(2)}) copy-start(bf16[64,512]{1,0:T(8,128)(2,1)} %get-tuple-element.5) | copy-start | bytes 196612

commit v4 on v3

--- a/solution.py
+++ b/solution.py
@@ -11,6 +11,7 @@
 HEADDIM = 64
 NSTATE = 128
 ROWS = 128
+SUB = 128
 RING = 4
 EPS = 1e-05
 F32 = jnp.float32
@@ -133,6 +134,7 @@
     half = piece // 2
     count = rows_r.shape[1]
     slots = chunks * ROWS
+    subs = ROWS // SUB
     cap = slots // readers
     tok_rows, part = tok_buf.shape
     my_cols = pl.ds(pl.multiple_of((2 * me + sec) * part, part), part)
@@ -325,8 +327,8 @@
         & (slot_r < readers * (start_col + rows_c))
     )
     ids_row = jnp.sum(jnp.where(held_c, ids_c, 0.0), axis=0, keepdims=True)
-    for t in range(chunks):
-        seg_row[t] = jnp.broadcast_to(ids_row[:, t * ROWS : (t + 1) * ROWS], (8, ROWS))
+    for k in range(slots // SUB):
+        seg_row[k] = jnp.broadcast_to(ids_row[:, k * SUB : (k + 1) * SUB], (8, SUB))
     slot_c = iota((slots, count), 0)
     held_r = (
         (own_r[...] == owner)
@@ -334,7 +336,7 @@
         & (slot_c < readers * (start_row + rows_r[...]))
     )
     ids_col = jnp.sum(jnp.where(held_r, ids_r, 0.0), axis=1, keepdims=True)
-    seg_col[...] = jnp.broadcast_to(ids_col, (slots, ROWS))
+    seg_col[...] = jnp.broadcast_to(ids_col, (slots, SUB))
     place, reader = slot_r % cap, slot_r // cap
     held = (own_c == owner) & (place >= start_col) & (place < start_col + rows_c)
     goal = jnp.sum(
@@ -344,7 +346,7 @@
     ) - 1
     state[...] = jnp.zeros_like(state)
     prev[...] = jnp.full(prev.shape, -1.0, F32)
-    lane = iota((ROWS, 128), 1)
+    lane = iota((SUB, 128), 1)
     low = lane < HEADDIM
 
     def spread(value, pair):
@@ -431,15 +433,17 @@
         )
         gate_buf[...] = silu(jnp.dot(normed[...], w_gate[...], preferred_element_type=F32))
 
-    def stage_scan(t):
-        segment_c = seg_col[rows_of(t), :]
-        segment_r = jnp.broadcast_to(seg_row[t][0:1, :], (ROWS, ROWS))
-        before = jnp.broadcast_to(prev[0:1, :], (ROWS, ROWS))
-        last = segment_c[ROWS - 1 : ROWS, :]
-        down, across = iota((ROWS, ROWS), 0), iota((ROWS, ROWS), 1)
+    def stage_scan(t, sub):
+        here = slice(sub * SUB, (sub + 1) * SUB)
+        rows = pl.ds(pl.multiple_of(t * ROWS + sub * SUB, SUB), SUB)
+        segment_c = seg_col[rows, :]
+        segment_r = jnp.broadcast_to(seg_row[t * subs + sub][0:1, :], (SUB, SUB))
+        before = jnp.broadcast_to(prev[0:1, :], (SUB, SUB))
+        last = segment_c[SUB - 1 : SUB, :]
+        down, across = iota((SUB, SUB), 0), iota((SUB, SUB), 1)
         causal = down >= across
         hidden = jnp.where(causal & (segment_c == segment_r), 0.0, -1e30)
-        dt = dt_buf[...]
+        dt = dt_buf[here, :]
         cum = jnp.dot(
             causal.astype(F32),
             dt * rate,
@@ -449,18 +453,18 @@
         cum_t, dt_t = cum.T, dt.T
         grown = jnp.exp(cum)
         from_before = jnp.where(segment_c == before, grown, 0.0)
-        last_cum = cum[ROWS - 1 : ROWS, :]
+        last_cum = cum[SUB - 1 : SUB, :]
         tail = jnp.where(segment_c == last, jnp.exp(last_cum - cum), 0.0) * dt
         kept = jnp.where(last == prev[0:1, :], jnp.exp(last_cum), 0.0)
-        b_rows, c_rows = bc_buf[:, :NSTATE], bc_buf[:, NSTATE:]
+        b_rows, c_rows = bc_buf[here, :NSTATE], bc_buf[here, NSTATE:]
         scores = lax.dot_general(
             c_rows, b_rows, (((1,), (1,)), ((), ())), preferred_element_type=F32
         )
         readout = jnp.dot(c_rows, state[...].astype(BF16), preferred_element_type=F32)
-        squares = jnp.zeros((ROWS, 128), F32)
+        squares = jnp.zeros((SUB, 128), F32)
         for pair in range(pairs):
             cols = slice(pair * 128, (pair + 1) * 128)
-            x_pair = xs_buf[:, cols]
+            x_pair = xs_buf[here, cols]
             x_f = x_pair.astype(F32)
             parts = []
             for head in (2 * pair, 2 * pair + 1):
@@ -472,16 +476,16 @@
                 + spread(from_before, pair) * readout[:, cols]
                 + skip_row[0:1, cols] * x_f
             )
-            gated = total * gate_buf[:, cols]
+            gated = total * gate_buf[here, cols]
             squares = squares + gated * gated
-            y_ref[rows_of(t), cols] = (gated * norm_gain[:, cols]).astype(BF16)
+            y_ref[rows, cols] = (gated * norm_gain[:, cols]).astype(BF16)
             scaled = (spread(tail, pair) * x_f).astype(BF16)
             fresh = lax.dot_general(
                 b_rows, scaled, (((0,), (0,)), ((), ())), preferred_element_type=F32
             )
             state[:, cols] = spread(kept, pair) * state[:, cols] + fresh
         prev[...] = jnp.broadcast_to(last, prev.shape)
-        sq_buf[0, t] = jnp.broadcast_to(jnp.sum(squares.T, axis=0, keepdims=True), (8, ROWS))
+        sq_buf[0, t, sub] = jnp.broadcast_to(jnp.sum(squares.T, axis=0, keepdims=True), (8, SUB))
 
     def square_copy(t, k):
         return push(
@@ -506,13 +510,15 @@
         )
 
     def gather_copy(t, k):
-        where, to = (
-            (lambda: out_piece(t, me), right),
-            (lambda: out_piece(t, me), left),
-            (lambda: out_piece(t, left, 0), right),
-            (lambda: out_piece(t, right, 1), left),
+        who, which, to = (
+            (me, 0, right),
+            (me, 1, left),
+            (me, 1, right),
+            (me, 0, left),
+            (left, 0, right),
+            (right, 1, left),
         )[k]
-        rows = o_buf.at[where()]
+        rows = o_buf.at[out_piece(t, who, which)]
         return push(rows, rows, ag_send.at[k, t], ag_recv.at[k, t], tensor=to)
 
     def stage_out(t):
@@ -534,7 +540,9 @@
             square_copy(t, k).wait_recv()
         total = sq_buf[0, t] + sq_buf[1, t] + sq_buf[2, t] + sq_buf[3, t]
         scale = lax.rsqrt(total / (RING * inner) + EPS)
-        rs_ref[rows_of(t), :] = jnp.broadcast_to(scale[0:1, :], (ROWS, ROWS)).T
+        for sub in range(subs):
+            rows = pl.ds(pl.multiple_of(t * ROWS + sub * SUB, SUB), SUB)
+            rs_ref[rows, :] = jnp.broadcast_to(scale[sub, 0:1, :], (SUB, SUB)).T
         yn_buf[rows_of(t), :] = (
             y_ref[rows_of(t), :].astype(F32) * rs_ref[rows_of(t), 0:1]
         ).astype(BF16)
@@ -550,19 +558,21 @@
             o_buf[where, :] = (
                 u_buf[where, :].astype(F32) + rs_ref[where, 0:1] * summed
             ).astype(BF16)
-        gather_copy(t, 0).start()
-        gather_copy(t, 1).start()
+        for k in range(4):
+            gather_copy(t, k).start()
         pass_on(t, 0)
 
     def gather_second(t):
         for k in (0, 1):
             gather_copy(t, k).wait_recv()
-            gather_copy(t, k + 2).start()
+            gather_copy(t, k + 4).start()
+        for k in (2, 3):
+            gather_copy(t, k).wait_recv()
         pass_on(t, 1, 2)
 
     def gather_last(t):
-        gather_copy(t, 2).wait_recv()
-        gather_copy(t, 3).wait_recv()
+        gather_copy(t, 4).wait_recv()
+        gather_copy(t, 5).wait_recv()
         pass_on(t, 3, 4)
         store_out(t).start()
 
@@ -626,45 +636,43 @@
                 exchange(m).start()
 
     def step(t, carry):
-        @pl.when(t >= 4)
-        def _():
-            gather_last(t - 4)
-
-        @pl.when((t >= 3) & (t < chunks + 3))
-        def _():
-            gather_second(t - 3)
-
-        @pl.when((t >= 2) & (t < chunks + 2))
-        def _():
-            reduce_last(t - 2)
-
         @pl.when(t < chunks)
         def _():
             stage_in(t)
-
-        @pl.when((t >= 1) & (t < chunks + 1))
-        def _():
-            reduce_second(t - 1)
-
-        @pl.when(t < chunks)
-        def _():
-            stage_scan(t)
+            for sub in range(subs):
+                stage_scan(t, sub)
             for k in range(1, RING):
                 square_copy(t, k).start()
             stage_out(t)
 
-        @pl.when(t == chunks)
+        @pl.when((t >= 1) & (t < chunks + 1))
+        def _():
+            reduce_second(t - 1)
+
+        @pl.when((t >= 2) & (t < chunks + 2))
+        def _():
+            reduce_last(t - 2)
+
+        @pl.when(t == chunks + 4 * (1 - sec))
         def _():
             lax.fori_loop(0, levels, grad_early, 0)
 
-        @pl.when(t == chunks + 1)
+        @pl.when(t == chunks + 1 + 3 * (1 - sec))
         def _():
             grad_send(0)
             grad_send(1)
 
-        return carry
-
-    lax.fori_loop(0, chunks + 4, step, 0)
+        @pl.when((t >= 3) & (t < chunks + 3))
+        def _():
+            gather_second(t - 3)
+
+        @pl.when((t >= 4) & (t < chunks + 4))
+        def _():
+            gather_last(t - 4)
+
+        return carry
+
+    lax.fori_loop(0, chunks + 4 + (1 - sec), step, 0)
     grad_second(0)
     grad_second(1)
     grad_finish(0)
@@ -691,7 +699,7 @@
     def drain(t, carry):
         for k in range(6):
             reduce_copy(t, k).wait_send()
-        for k in range(4):
+        for k in range(6):
             gather_copy(t, k).wait_send()
         for k in range(1, RING):
             square_copy(t, k).wait_send()
@@ -748,11 +756,11 @@
         functools.partial(block_kernel, chunks, heads, levels),
         name="blocks",
         out_shape=(
-            jax.ShapeDtypeStruct((slots, width), BF16),
-            jax.ShapeDtypeStruct((share, inner), BF16),
+            pltpu.VMEM((slots, width), BF16),
+            pltpu.VMEM((share, inner), BF16),
         ),
         in_specs=[vmem] * 8 + [anywhere] * 6,
-        out_specs=(anywhere, vmem),
+        out_specs=(vmem, vmem),
         scratch_shapes=[
             pltpu.VMEM((width, inner), BF16),
             pltpu.VMEM((width, inner), BF16),
@@ -783,8 +791,8 @@
             pltpu.VMEM((NSTATE, inner), F32),
             pltpu.VMEM((8, 128), F32),
             pltpu.VMEM((slots, 128), F32),
-            pltpu.VMEM((chunks, 8, 128), F32),
-            pltpu.VMEM((RING, chunks, 8, 128), F32),
+            pltpu.VMEM((slots // SUB, 8, 128), F32),
+            pltpu.VMEM((RING, chunks, ROWS // SUB, 8, 128), F32),
             pltpu.VMEM((8, inner), F32),
             pltpu.VMEM((slots, width), BF16),
             pltpu.VMEM((levels, RING * share, slots), BF16),
@@ -809,8 +817,8 @@
             dma((chunks,)),
             dma((6, chunks)),
             dma((6, chunks)),
-            dma((4, chunks)),
-            dma((4, chunks)),
+            dma((6, chunks)),
+            dma((6, chunks)),
             dma((3, chunks)),
             dma((3, chunks)),
             dma((6, 2)),

time: 106 us -> 96.7 us (0.912)
  Pallas kernels: 102 us -> 94 us
  local copies, waits for them, and re-layouts: 3.82 us -> 1.95 us
    pallas_call x1, Pallas kernels: 102 us -> 94 us  [run_blocks(): pl.pallas_call(functools.partial(block_kernel, chunks, heads, levels), na...]
    unnamed x4 -> x2, local copies, waits for them, and re-layouts: 3.82 us -> 1.95 us
where the time goes in v4:
time: 96.7 us; the launch traced here: 96.5 us
  Pallas kernels  94 us (97%)
  local copies, waits for them, and re-layouts  1.95 us (2%)
    pallas_call x1, Pallas kernels, run_blocks(): pl.pallas_call(functools.partial(block_kernel, chunks, heads, levels), na...  94 us
    unnamed x2, local copies, waits for them, and re-layouts  1.95 us

profile of v4, /device:TPU:1, one launch (start us, length us, event | category | flops | bytes accessed | tf_op | source)
XLA Modules:
  0.0 96.5 jit_solution(13923230295931077271)
XLA Ops:
  0.6 94.0 %blocks.1 = (bf16[512,2048]{1,0:T(8,128)(2,1)S(1)}, bf16[64,512]{1,0:T(8,128)(2,1)S(1)}) custom-call(s32[1,128]{1,0:T(1,128)} %bitcast.22, s32[1,128]{1,0:T(1,128)} %bitcast.23, f32[1,2048]{1,0:T(1,128)} %pre_gain.1, f32[1,8]{1,0:T(1,128)} %step_bias.1, f32[1,8]{1,0:T(1,128)} %decay_log.1, f32[1,8]{1,0:T(1,128)} %skip_gain.1, f32[1,512]{1,0:T(1,128)} %norm_gain.1, ...), custom_call_target="tpu_custom_call" | custom-call | tf_op jit(solution)/shard_map/blocks/pallas_call | solution.py:755
  94.6 1.3 %copy.18 = bf16[1,512,2048]{2,1,0:T(8,128)(2,1)} copy(bf16[1,512,2048]{2,1,0:T(8,128)(2,1)S(1)} %bitcast.14) | data formatting | bytes 4194304
  95.9 0.6 copy.19

commit v5 on v4

--- a/solution.py
+++ b/solution.py
@@ -69,7 +69,6 @@
     away,
     arrived,
     s_buf,
-    r_buf,
     u_buf,
     o_buf,
     p_buf,
@@ -105,10 +104,6 @@
     turn_send,
     turn_recv,
     feed_send,
-    side_recv,
-    relay_send,
-    relay_recv,
-    fill_send,
     hand_sem,
     hand_send,
     out_sem,
@@ -220,58 +215,15 @@
     def feed_own(t):
         return pltpu.make_async_copy(s_buf.at[t], u_buf.at[rows_of(t), my_cols], hand_sem.at[t])
 
-    def feed_core(t):
+    def feed(t, k):
         return push(
             s_buf.at[t],
             u_buf.at[rows_of(t), my_cols],
-            feed_send.at[2, t],
+            feed_send.at[k, t],
             hand_sem.at[t],
             section=0,
-        )
-
-    def feed_side(t, k):
-        return push(
-            s_buf.at[t],
-            r_buf.at[t, :, my_cols],
-            feed_send.at[k, t],
-            side_recv.at[k, t],
-            section=1,
-            tensor=(right, left)[k],
-        )
-
-    def held_of(t, k, kind):
-        near, far = (left, right)[k], opposite
-        half_rows = pl.ds(k * (ROWS // 2), ROWS // 2)
-        who = far if kind == 2 else near
-        cols = pl.ds(pl.multiple_of(who * 2 * part, 2 * part), 2 * part)
-        if kind == 0:
-            return r_buf.at[t, :, cols], u_buf.at[rows_of(t), cols]
-        there = pl.ds(pl.multiple_of(t * ROWS + k * (ROWS // 2), ROWS // 2), ROWS // 2)
-        return r_buf.at[t, half_rows, cols], u_buf.at[there, cols]
-
-    def relay(t, k):
-        src, _ = held_of(t, k, 1)
-        return push(
-            src, src, relay_send.at[k, t], relay_recv.at[k, t], tensor=(right, left)[k]
-        )
-
-    def fill(t, k, kind):
-        src, dst = held_of(t, k, kind)
-        return push(src, dst, fill_send.at[k + kind, t], hand_sem.at[t], section=0)
-
-    def sides(t, carry):
-        for k in (0, 1):
-            here, _ = held_of(t, k, 0)
-            pltpu.make_async_copy(here, here, side_recv.at[k, t]).wait()
-            relay(t, k).start()
-            fill(t, k, 0).start()
-        return carry
-
-    def relayed(t, carry):
-        for k in (0, 1):
-            relay(t, k).wait_recv()
-            fill(t, k, 2).start()
-        return carry
+            tensor=(me + k) % RING,
+        )
 
     def hand_over(t, k):
         where = (
@@ -387,8 +339,8 @@
     for t in range(chunks):
         placed = (iota((ROWS, slots), 0) + t * ROWS == goal).astype(F32).astype(BF16)
         s_buf[t] = jnp.dot(placed, arrived[...], preferred_element_type=F32).astype(BF16)
-        feed_side(t, 0).start()
-        feed_side(t, 1).start()
+        for k in (2, 1, 3):
+            feed(t, k).start()
 
         @pl.when(sec == 0)
         def _():
@@ -396,22 +348,7 @@
 
         @pl.when(sec == 1)
         def _():
-            feed_core(t).start()
-
-    @pl.when(sec == 1)
-    def _():
-        def relay_step(t, carry):
-            @pl.when(t < chunks)
-            def _():
-                sides(t, 0)
-
-            @pl.when(t >= 1)
-            def _():
-                relayed(t - 1, 0)
-
-            return carry
-
-        lax.fori_loop(0, chunks + 1, relay_step, 0)
+            feed(t, 0).start()
 
     for load in loads[1:5]:
         load.wait()
@@ -703,8 +640,7 @@
             gather_copy(t, k).wait_send()
         for k in range(1, RING):
             square_copy(t, k).wait_send()
-        feed_side(t, 0).wait_send()
-        feed_side(t, 1).wait_send()
+            feed(t, k).wait_send()
 
         @pl.when(sec == 0)
         def _():
@@ -713,11 +649,7 @@
 
         @pl.when(sec == 1)
         def _():
-            feed_core(t).wait_send()
-            for k in (0, 1):
-                relay(t, k).wait_send()
-                fill(t, k, 0).wait_send()
-                fill(t, k, 2).wait_send()
+            feed(t, 0).wait_send()
 
         store_out(t).wait()
         return carry
@@ -772,7 +704,6 @@
             pltpu.VMEM((slots, part), BF16),
             pltpu.VMEM((slots, part), BF16),
             pltpu.VMEM((chunks, ROWS, part), BF16),
-            pltpu.VMEM((chunks, ROWS, width), BF16),
             pltpu.VMEM((slots, width), BF16),
             pltpu.VMEM((slots, width), BF16),
             pltpu.VMEM((chunks, ROWS, width), BF16),
@@ -807,11 +738,7 @@
             dma((6,)),
             dma((readers,)),
             dma((readers,)),
-            dma((3, chunks)),
-            dma((2, chunks)),
-            dma((2, chunks)),
-            dma((2, chunks)),
-            dma((4, chunks)),
+            dma((RING, chunks)),
             dma((chunks,)),
             dma((5, chunks)),
             dma((chunks,)),

time: 96.7 us -> 94.9 us (0.981)
  Pallas kernels: 94 us -> 92.1 us
    pallas_call x1, Pallas kernels: 94 us -> 92.1 us  [run_blocks(): pl.pallas_call(functools.partial(block_kernel, chunks, heads, levels), na...]
where the time goes in v5:
time: 94.9 us; the launch traced here: 94.7 us
  Pallas kernels  92.1 us (97%)
  local copies, waits for them, and re-layouts  1.95 us (2%)
    pallas_call x1, Pallas kernels, run_blocks(): pl.pallas_call(functools.partial(block_kernel, chunks, heads, levels), na...  92.1 us
    unnamed x2, local copies, waits for them, and re-layouts  1.95 us

profile of v5, /device:TPU:1, one launch (start us, length us, event | category | flops | bytes accessed | tf_op | source)
XLA Modules:
  0.0 94.7 jit_solution(11704725370563341127)
XLA Ops:
  0.6 92.1 %blocks.1 = (bf16[512,2048]{1,0:T(8,128)(2,1)S(1)}, bf16[64,512]{1,0:T(8,128)(2,1)S(1)}) custom-call(s32[1,128]{1,0:T(1,128)} %bitcast.22, s32[1,128]{1,0:T(1,128)} %bitcast.23, f32[1,2048]{1,0:T(1,128)} %pre_gain.1, f32[1,8]{1,0:T(1,128)} %step_bias.1, f32[1,8]{1,0:T(1,128)} %decay_log.1, f32[1,8]{1,0:T(1,128)} %skip_gain.1, f32[1,512]{1,0:T(1,128)} %norm_gain.1, ...), custom_call_target="tpu_custom_call" | custom-call | tf_op jit(solution)/shard_map/blocks/pallas_call | solution.py:687
  92.8 1.3 %copy.18 = bf16[1,512,2048]{2,1,0:T(8,128)(2,1)} copy(bf16[1,512,2048]{2,1,0:T(8,128)(2,1)S(1)} %bitcast.14) | data formatting | bytes 4194304
  94.1 0.6 copy.19

commit v6 on v5

--- a/solution.py
+++ b/solution.py
@@ -153,8 +153,7 @@
             )
         )
     ]
-    for load in loads:
-        load.start()
+    loads[0].start()
 
     barrier = pltpu.get_barrier_semaphore()
 
@@ -260,15 +259,22 @@
     )
     chosen = (iota((slots, tok_rows), 0) == target).astype(F32).astype(BF16)
     loads[0].wait()
+    for load in loads[1:]:
+        load.start()
     away[...] = jnp.dot(chosen, tok_buf[...], preferred_element_type=F32).astype(BF16)
     arrived[cap_of(owner), :] = away[cap_of(owner), :]
     pl.semaphore_wait(barrier, readers - 1 + RING - 1 + RING)
 
     def send_turn(k, carry):
-        turn(k).start()
+        far = (k + readers // 2) % readers
+
+        @pl.when(far != 0)
+        def _():
+            turn(far).start()
+
         return carry
 
-    lax.fori_loop(1, readers, send_turn, 0)
+    lax.fori_loop(0, readers, send_turn, 0)
 
     ids_c = (iota((count, 1), 0) + 1).astype(F32)
     ids_r = (iota((1, count), 1) + 1).astype(F32)

time: 94.9 us -> 94.1 us (level)
  no operation moved by 1% of the time
where the time goes in v6:
time: 94.1 us; the launch traced here: 93.9 us
  Pallas kernels  91.4 us (97%)
  local copies, waits for them, and re-layouts  1.95 us (2%)
    pallas_call x1, Pallas kernels, run_blocks(): pl.pallas_call(functools.partial(block_kernel, chunks, heads, levels), na...  91.4 us
    unnamed x2, local copies, waits for them, and re-layouts  1.95 us

profile of v6, /device:TPU:1, one launch (start us, length us, event | category | flops | bytes accessed | tf_op | source)
XLA Modules:
  0.0 93.9 jit_solution(16270377461921359526)
XLA Ops:
  0.6 91.4 %blocks.1 = (bf16[512,2048]{1,0:T(8,128)(2,1)S(1)}, bf16[64,512]{1,0:T(8,128)(2,1)S(1)}) custom-call(s32[1,128]{1,0:T(1,128)} %bitcast.22, s32[1,128]{1,0:T(1,128)} %bitcast.23, f32[1,2048]{1,0:T(1,128)} %pre_gain.1, f32[1,8]{1,0:T(1,128)} %step_bias.1, f32[1,8]{1,0:T(1,128)} %decay_log.1, f32[1,8]{1,0:T(1,128)} %skip_gain.1, f32[1,512]{1,0:T(1,128)} %norm_gain.1, ...), custom_call_target="tpu_custom_call" | custom-call | tf_op jit(solution)/shard_map/blocks/pallas_call | solution.py:693
  92.0 1.3 %copy.18 = bf16[1,512,2048]{2,1,0:T(8,128)(2,1)} copy(bf16[1,512,2048]{2,1,0:T(8,128)(2,1)S(1)} %bitcast.14) | data formatting | bytes 4194304
  93.3 0.6 copy.19

commit v7 on v6

--- a/solution.py
+++ b/solution.py
@@ -573,7 +573,7 @@
     def grad_finish(g):
         for k in range(2, 6):
             grad_copy(g, k).wait_recv()
-        for m in range(g * group, (g + 1) * group):
+        for m in ((2, 1, 3, 0), (4, 7, 5))[g]:
             if m != levels - 2:
                 h_buf[m] = level_sum(m).astype(BF16)
                 exchange(m).start()
@@ -609,14 +609,17 @@
         def _():
             gather_second(t - 3)
 
+        @pl.when(t == chunks + 2 + 3 * (1 - sec))
+        def _():
+            grad_second(0)
+
         @pl.when((t >= 4) & (t < chunks + 4))
         def _():
             gather_last(t - 4)
 
         return carry
 
-    lax.fori_loop(0, chunks + 4 + (1 - sec), step, 0)
-    grad_second(0)
+    lax.fori_loop(0, chunks + 4 + 2 * (1 - sec), step, 0)
     grad_second(1)
     grad_finish(0)
     grad_finish(1)

time: 94.1 us -> 94.8 us (level)
  no operation moved by 1% of the time
where the time goes in v7:
time: 94.8 us; the launch traced here: 94.6 us
  Pallas kernels  92 us (97%)
  local copies, waits for them, and re-layouts  1.95 us (2%)
    pallas_call x1, Pallas kernels, run_blocks(): pl.pallas_call(functools.partial(block_kernel, chunks, heads, levels), na...  92 us
    unnamed x2, local copies, waits for them, and re-layouts  1.95 us

profile of v7, /device:TPU:1, one launch (start us, length us, event | category | flops | bytes accessed | tf_op | source)
XLA Modules:
  0.0 94.6 jit_solution(6550825268847323909)
XLA Ops:
  0.6 92.0 %blocks.1 = (bf16[512,2048]{1,0:T(8,128)(2,1)S(1)}, bf16[64,512]{1,0:T(8,128)(2,1)S(1)}) custom-call(s32[1,128]{1,0:T(1,128)} %bitcast.22, s32[1,128]{1,0:T(1,128)} %bitcast.23, f32[1,2048]{1,0:T(1,128)} %pre_gain.1, f32[1,8]{1,0:T(1,128)} %step_bias.1, f32[1,8]{1,0:T(1,128)} %decay_log.1, f32[1,8]{1,0:T(1,128)} %skip_gain.1, f32[1,512]{1,0:T(1,128)} %norm_gain.1, ...), custom_call_target="tpu_custom_call" | custom-call | tf_op jit(solution)/shard_map/blocks/pallas_call | solution.py:696
  92.7 1.3 %copy.18 = bf16[1,512,2048]{2,1,0:T(8,128)(2,1)} copy(bf16[1,512,2048]{2,1,0:T(8,128)(2,1)S(1)} %bitcast.14) | data formatting | bytes 4194304
  94.0 0.6 copy.19

commit v8 on v6

--- a/solution.py
+++ b/solution.py
@@ -515,8 +515,9 @@
 
     def gather_last(t):
         gather_copy(t, 4).wait_recv()
+        pass_on(t, 3)
         gather_copy(t, 5).wait_recv()
-        pass_on(t, 3, 4)
+        pass_on(t, 4)
         store_out(t).start()
 
     early = (chunks - 1) * ROWS

time: 94.1 us -> 94.7 us (level)
  no operation moved by 1% of the time
where the time goes in v8:
time: 94.7 us; the launch traced here: 94.5 us
  Pallas kernels  91.9 us (97%)
  local copies, waits for them, and re-layouts  1.95 us (2%)
    pallas_call x1, Pallas kernels, run_blocks(): pl.pallas_call(functools.partial(block_kernel, chunks, heads, levels), na...  91.9 us
    unnamed x2, local copies, waits for them, and re-layouts  1.95 us

profile of v8, /device:TPU:1, one launch (start us, length us, event | category | flops | bytes accessed | tf_op | source)
XLA Modules:
  0.0 94.5 jit_solution(12397328426834764691)
XLA Ops:
  0.6 91.9 %blocks.1 = (bf16[512,2048]{1,0:T(8,128)(2,1)S(1)}, bf16[64,512]{1,0:T(8,128)(2,1)S(1)}) custom-call(s32[1,128]{1,0:T(1,128)} %bitcast.22, s32[1,128]{1,0:T(1,128)} %bitcast.23, f32[1,2048]{1,0:T(1,128)} %pre_gain.1, f32[1,8]{1,0:T(1,128)} %step_bias.1, f32[1,8]{1,0:T(1,128)} %decay_log.1, f32[1,8]{1,0:T(1,128)} %skip_gain.1, f32[1,512]{1,0:T(1,128)} %norm_gain.1, ...), custom_call_target="tpu_custom_call" | custom-call | tf_op jit(solution)/shard_map/blocks/pallas_call | solution.py:694
  92.5 1.3 %copy.18 = bf16[1,512,2048]{2,1,0:T(8,128)(2,1)} copy(bf16[1,512,2048]{2,1,0:T(8,128)(2,1)S(1)} %bitcast.14) | data formatting | bytes 4194304
  93.9 0.6 copy.19
